TPU v7x, 512 devices: a whole 4x8x8 slice. The times are simulated.
512 devices in a mesh: slab: 128 (over z, x, y_lo), sec: 4 (over y_hi, core).
Axes of the slice: x: 4, y: 8 (y_hi: 2, y_lo: 4; y = y_hi * 4 + y_lo), z: 8, core: 2. Of those that a mesh axis runs over, the one named last changes fastest.
Arguments:
- displacement: float32 [5120, 4096], P('slab', 'sec'), may hold values from -6 to 6
- earlier_field: float32 [5120, 4096], P('slab', 'sec'), may hold values from -6 to 6
- region_ids: int32 [4096], P('sec'), may hold values from 0 to 7
- material: float32 [2, 8], replicated, may hold values from 0.5 to 1.5
- mode_shapes: float32 [4096, 64], P('sec'), may hold values from -0.75 to 0.75
- band_edges: int32 [2, 64], replicated, may hold values from 0 to 4095, as said below
Outputs:
- advanced_field: float32 [5120, 4096], P('slab', 'sec')
- band_field: bfloat16 [5120, 4096], P('slab', 'sec')
Inputs may be any that keep to these rules, and one draw needn't show every extreme that they name: `band_edges`: for every mode the lower edge is below the upper edge; some mode's band starts at 0 and some mode's band ends at 4095.
All inputs are finite; a program needn't handle non-finite values.
Results may differ from a plain program's by a relative error of at most 0.001.
Values sent between devices are 32-bit elements; how exact they have to be, the bound alone decides.
A program may use at most 64 MiB of HBM per device.

v0:
```python
import math

import jax
import jax.numpy as jnp
from jax import lax
from jax.sharding import PartitionSpec as P

COLS = 64
MODES = 64
WAVES = 4096
REGIONS = 8
STEPS = 4


courant_sq = 0.14
two_pi = 2.0 * math.pi


def extended_2(x, sides, width, wrap):
    for axis, dim in sides:
        peers, length = (lax.axis_size(axis), x.shape[dim])
        up = [(i, (i + 1) % peers) for i in range(peers if wrap else peers - 1)]
        down = [(j, i) for i, j in up]
        last = lax.slice_in_dim(x, length - width, length, axis=dim)
        leading = lax.slice_in_dim(x, 0, width, axis=dim)
        before = lax.ppermute(last, axis, up)
        after = lax.ppermute(leading, axis, down)
        x = jnp.concatenate([before, x, after], axis=dim)
    return x


def lookup_stiffness(region_ids, material):
    values = courant_sq * material[0] * material[1]
    match = region_ids[:, None] == jnp.arange(REGIONS, dtype=jnp.int32)[None, :]
    return jnp.sum(jnp.where(match, values[None, :], jnp.zeros_like(values)[None, :]), axis=1)


def advance(extended, before, stiffness):
    centre = extended[1:-1]
    cells_here = centre.shape[1]
    widened = extended_2(centre, (("sec", 1),), COLS, False)
    above = widened[:, :cells_here]
    below = widened[:, 2 * COLS :]
    planar = centre.reshape(centre.shape[0], cells_here // COLS, COLS)
    west_cells = jnp.pad(planar[:, :, :-1], ((0, 0), (0, 0), (1, 0))).reshape(centre.shape)
    east_cells = jnp.pad(planar[:, :, 1:], ((0, 0), (0, 0), (0, 1))).reshape(centre.shape)
    summed = extended[2:] + extended[:-2] + above + below + west_cells + east_cells
    return 2.0 * centre - before + stiffness[None, :] * (summed - 6.0 * centre)


def phases(first, second, period_len):
    product = first[:, None] * second[None, :]
    return (product % period_len).astype(jnp.float32) * (two_pi / period_len)


def body(displacement, earlier_field, region_ids, material, mode_shapes, band_edges):
    planes_here = displacement.shape[0]
    period_len = planes_here * lax.axis_size("slab")
    stiffness = lookup_stiffness(region_ids, material)
    current, before = (displacement, earlier_field)
    for _ in range(STEPS):
        extended = extended_2(current, (("slab", 0),), 1, True)
        current, before = (advance(extended, before, stiffness), current)
    modal_part = jnp.dot(current, mode_shapes, precision=lax.Precision.HIGHEST)
    plane_ids = lax.axis_index("slab") * planes_here + jnp.arange(planes_here, dtype=jnp.int32)
    lower_edge = jnp.concatenate([band_edges[0], band_edges[0]])[None, :]
    upper_edge = jnp.concatenate([band_edges[1], band_edges[1]])[None, :]
    empty = jnp.zeros((planes_here, MODES), jnp.float32)
    modal = lax.psum(modal_part, "sec")
    owned_rows = WAVES // lax.axis_size("slab")
    row_count = owned_rows * lax.axis_size("slab")
    block_len = min(row_count, 512)

    def make_one_block(index):
        wavenums = index * block_len + jnp.arange(block_len, dtype=jnp.int32)
        angle = phases(wavenums, plane_ids, period_len)
        return jnp.concatenate(
            [
                jnp.dot(jnp.cos(angle), modal, precision=lax.Precision.HIGHEST),
                jnp.dot(jnp.sin(angle), modal, precision=lax.Precision.HIGHEST),
            ],
            axis=1,
        )

    result = lax.map(make_one_block, jnp.arange(row_count // block_len, dtype=jnp.int32))
    owned = lax.psum_scatter(
        result.reshape(row_count, 2 * MODES), "slab", scatter_dimension=0, tiled=True
    )
    wavenums = (
        lax.axis_index("slab") * owned_rows + jnp.arange(owned.shape[0], dtype=jnp.int32)[:, None]
    )
    in_band = (wavenums >= lower_edge) & (wavenums < upper_edge)
    filtered = jnp.where(in_band, owned, jnp.zeros_like(owned))
    running = empty
    portion = lax.all_gather(filtered, "slab", axis=0, tiled=True)
    row_count = portion.shape[0]
    inverse_block_len = min(row_count, 512)
    portions = portion.reshape(row_count // inverse_block_len, inverse_block_len, 2 * MODES)

    def inverse_one_block(inner, item):
        index, piece_rows = item
        wavenums = index * inverse_block_len + jnp.arange(inverse_block_len, dtype=jnp.int32)
        angle = phases(plane_ids, wavenums, period_len)
        inner = inner + jnp.dot(
            jnp.cos(angle), piece_rows[:, :MODES], precision=lax.Precision.HIGHEST
        )
        inner = inner + jnp.dot(
            jnp.sin(angle), piece_rows[:, MODES:], precision=lax.Precision.HIGHEST
        )
        return (inner, None)

    running, _ = lax.scan(
        inverse_one_block,
        running,
        (jnp.arange(row_count // inverse_block_len, dtype=jnp.int32), portions),
    )
    smooth = running
    smooth = smooth * (2.0 / period_len)
    band_field = jnp.dot(smooth, mode_shapes.T, precision=lax.Precision.HIGHEST).astype(
        jnp.bfloat16
    )
    return (current, band_field)


def solution(mesh):
    return jax.shard_map(
        body,
        mesh=mesh,
        in_specs=(P("slab", "sec"), P("slab", "sec"), P("sec"), P(), P("sec", None), P()),
        out_specs=(P("slab", "sec"), P("slab", "sec")),
        check_vma=False,
    )
```

profile of v0, /device:TPU:32, one launch (start us, length us, event | category | flops | bytes accessed | tf_op | source)
XLA Modules:
  0.0 1638.3 jit_solution(503849871708262057)
XLA Ops:
  8.1 1.9 collective-permute-start.2
  10.1 7.5 collective-permute-start.3
  18.4 13.5 collective-permute-start
  31.9 1.9 collective-permute-start.1
  37.0 6.4 collective-permute-done.1
  43.8 1.9 collective-permute-start.6
  45.7 7.5 collective-permute-start.7
  53.3 3.6 collective-permute-start.4
  56.9 2.2 collective-permute-start.5
  59.8 8.8 collective-permute-done.5
  68.9 1.9 collective-permute-start.10
  70.9 7.5 collective-permute-start.11
  78.4 1.9 collective-permute-start.8
  80.4 3.9 collective-permute-start.9
  84.9 6.9 collective-permute-done.9
  92.3 1.9 collective-permute-start.14
  94.2 7.5 collective-permute-start.15
  101.7 1.9 collective-permute-start.12
  103.7 3.9 collective-permute-start.13
  108.2 6.9 collective-permute-done.13
  115.7 18.1 %psum.7 = f32[40,64]{1,0:T(8,128)S(1)} all-reduce(f32[40,64]{1,0:T(8,128)S(1)} %fusion.105), channel_id=1, replica_groups=mesh['slab'=128,'sec'=4] {'sec'}, use_global_device_ids=true, to_apply=%region_1.2 | all-reduce | flops 2560 | bytes 20480 | tf_op jit(solution)/shard_map/psum | solution.py:69
  133.8 41.0 %while.26 = (s32[]{:T(128)}, f32[8,512,128]{2,1,0:T(8,128)}, s32[8]{0:T(128)S(1)}, f32[40,64]{1,0:T(8,128)S(1)}, s32[]{:T(128)}, /*index=5*/s32[]{:T(128)}, s32[1]{0:T(128)}) while((s32[]{:T(128)}, f32[8,512,128]{2,1,0:T(8,128)}, s32[8]{0:T(128)S(1)}, f32[40,64]{1,0:T(8,128)S(1)}, s32[]{:T(128)}, /*index=5*/s32[]{:T(128)}, ...), condition=%wide.region_3.4_spmd.clone, body=%wide.region_2.3_spmd.clone.sunk | while | flops 31892012 | bytes 1862733 | solution.py:85
  135.2 1.5 fusion.125
  140.3 1.5 fusion.125
  145.4 1.5 fusion.125
  155.7 1.5 fusion.125
  160.8 1.5 fusion.125
  165.9 1.5 fusion.125
  171.1 1.5 fusion.125
  175.6 738.4 %reduce-scatter.2.cloned.1.call-done = f32[32,128]{1,0:T(8,128)} async-done(((f32[4096,128]{1,0:T(8,128)}), f32[32,128]{1,0:T(8,128)}) %reduce-scatter.2.cloned.1.call-update) | async-done | bytes 16400 | tf_op jit(solution)/shard_map/reduce_scatter | solution.py:86
  915.5 686.4 %all-gather.2.cloned.1.call-done = f32[4096,128]{1,0:T(8,128)} async-done(((f32[32,128]{1,0:T(8,128)}), f32[4096,128]{1,0:T(8,128)}) %all-gather.2.cloned.1.call-update) | async-done | bytes 2097168 | tf_op jit(solution)/shard_map/all_gather | solution.py:95
  1601.9 28.6 %while.27 = (s32[]{:T(128)}, f32[40,64]{1,0:T(8,128)S(1)}, s32[8]{0:T(128)S(1)}, f32[8,512,128]{2,1,0:T(8,128)}, s32[]{:T(128)}, /*index=5*/s32[]{:T(128)}, s32[1]{0:T(128)}, s32[]{:T(128)}) while((s32[]{:T(128)}, f32[40,64]{1,0:T(8,128)S(1)}, s32[8]{0:T(128)S(1)}, f32[8,512,128]{2,1,0:T(8,128)}, s32[]{:T(128)}, ...), condition=%wide.region_6.7_spmd.clone, body=%wide.region_5.6_spmd.clone.sunk | while | flops 31834156 | bytes 1096291 | solution.py:112
  (179 shorter events, 59.6 us)
Async XLA Ops:
  7.2 108.2 %copy-start = (f32[1024,64]{0,1:T(8,128)S(1)}, f32[1024,64]{0,1:T(8,128)}, u32[]{:S(2)}) copy-start(f32[1024,64]{0,1:T(8,128)} %param.14) | copy-start | bytes 786436
  7.2 36.2 %copy-start.1 = (f32[40,1024]{1,0:T(8,128)S(1)}, f32[40,1024]{1,0:T(8,128)}, u32[]{:S(2)}) copy-start(f32[40,1024]{1,0:T(8,128)} %param.10) | copy-start | bytes 491524
  7.2 36.2 %copy-start.3 = (f32[40,1024]{1,0:T(8,128)S(1)}, f32[40,1024]{1,0:T(8,128)}, u32[]{:S(2)}) copy-start(f32[40,1024]{1,0:T(8,128)} %param.11) | copy-start | bytes 491524
  7.2 906.9 %reduce-scatter.2.cloned.1.call-start = ((), (), s32[]{:S(2)}) async-start(), calls=%async_computation.1 | async-start | bytes 2113536 | tf_op jit(solution)/shard_map/reduce_scatter | solution.py:86
  8.1 35.3 %collective-permute-start.2 = (f32[40,64]{1,0:T(8,128)S(1)}, f32[40,64]{1,0:T(8,128)S(1)}, u32[]{:S(2)}, u32[]{:S(2)}) collective-permute-start(f32[40,64]{1,0:T(8,128)S(1)} %get-tuple-element.212), channel_id=1, source_target_pairs={{0,1},{1,2},{2,3},{4,5},{5,6},{6,7},{8,9},{9,10},{10,11},{12,13},{... | collective-permute-start | bytes 30728 | tf_op jit(solution)/shard_map/ppermute | solution.py:26
  10.1 33.3 %collective-permute-start.3 = (f32[40,64]{1,0:T(8,128)S(1)}, f32[40,64]{1,0:T(8,128)S(1)}, u32[]{:S(2)}, u32[]{:S(2)}) collective-permute-start(f32[40,64]{1,0:T(8,128)S(1)} %get-tuple-element.213), channel_id=1, source_target_pairs={{1,0},{2,1},{3,2},{5,4},{6,5},{7,6},{9,8},{10,9},{11,10},{13,12},{... | collective-permute-start | bytes 30728 | tf_op jit(solution)/shard_map/ppermute | solution.py:27
  18.4 18.6 %collective-permute-start = (f32[1,1024]{1,0:T(1,128)S(1)}, f32[1,1024]{1,0:T(1,128)S(1)}, u32[]{:S(2)}, u32[]{:S(2)}) collective-permute-start(f32[1,1024]{1,0:T(1,128)S(1)} %get-tuple-element.210), channel_id=1, source_target_pairs={{4,0},{8,4},{12,8},{16,12},{20,16},{24,20},{28,24},{32,28},{36,32}... | collective-permute-start | bytes 12296 | tf_op jit(solution)/shard_map/ppermute | solution.py:27
  31.9 11.5 collective-permute-start.1
  43.8 24.8 %collective-permute-start.6 = (f32[40,64]{1,0:T(8,128)S(1)}, f32[40,64]{1,0:T(8,128)S(1)}, u32[]{:S(2)}, u32[]{:S(2)}) collective-permute-start(f32[40,64]{1,0:T(8,128)S(1)} %get-tuple-element.208), channel_id=1, source_target_pairs={{0,1},{1,2},{2,3},{4,5},{5,6},{6,7},{8,9},{9,10},{10,11},{12,13},{... | collective-permute-start | bytes 30728 | tf_op jit(solution)/shard_map/ppermute | solution.py:26
  45.7 22.8 %collective-permute-start.7 = (f32[40,64]{1,0:T(8,128)S(1)}, f32[40,64]{1,0:T(8,128)S(1)}, u32[]{:S(2)}, u32[]{:S(2)}) collective-permute-start(f32[40,64]{1,0:T(8,128)S(1)} %get-tuple-element.209), channel_id=1, source_target_pairs={{1,0},{2,1},{3,2},{5,4},{6,5},{7,6},{9,8},{10,9},{11,10},{13,12},{... | collective-permute-start | bytes 30728 | tf_op jit(solution)/shard_map/ppermute | solution.py:27
  53.3 6.5 collective-permute-start.4
  56.9 11.7 collective-permute-start.5
  68.9 22.9 %collective-permute-start.10 = (f32[40,64]{1,0:T(8,128)S(1)}, f32[40,64]{1,0:T(8,128)S(1)}, u32[]{:S(2)}, u32[]{:S(2)}) collective-permute-start(f32[40,64]{1,0:T(8,128)S(1)} %get-tuple-element.204), channel_id=1, source_target_pairs={{0,1},{1,2},{2,3},{4,5},{5,6},{6,7},{8,9},{9,10},{10,11},{12,13},{... | collective-permute-start | bytes 30728 | tf_op jit(solution)/shard_map/ppermute | solution.py:26
  70.9 21.0 %collective-permute-start.11 = (f32[40,64]{1,0:T(8,128)S(1)}, f32[40,64]{1,0:T(8,128)S(1)}, u32[]{:S(2)}, u32[]{:S(2)}) collective-permute-start(f32[40,64]{1,0:T(8,128)S(1)} %get-tuple-element.205), channel_id=1, source_target_pairs={{1,0},{2,1},{3,2},{5,4},{6,5},{7,6},{9,8},{10,9},{11,10},{13,12},{... | collective-permute-start | bytes 30728 | tf_op jit(solution)/shard_map/ppermute | solution.py:27
  78.4 6.5 collective-permute-start.8
  80.4 11.5 collective-permute-start.9
  92.3 22.9 %collective-permute-start.14 = (f32[40,64]{1,0:T(8,128)S(1)}, f32[40,64]{1,0:T(8,128)S(1)}, u32[]{:S(2)}, u32[]{:S(2)}) collective-permute-start(f32[40,64]{1,0:T(8,128)S(1)} %get-tuple-element.200), channel_id=1, source_target_pairs={{0,1},{1,2},{2,3},{4,5},{5,6},{6,7},{8,9},{9,10},{10,11},{12,13},{... | collective-permute-start | bytes 30728 | tf_op jit(solution)/shard_map/ppermute | solution.py:26
  94.2 21.0 %collective-permute-start.15 = (f32[40,64]{1,0:T(8,128)S(1)}, f32[40,64]{1,0:T(8,128)S(1)}, u32[]{:S(2)}, u32[]{:S(2)}) collective-permute-start(f32[40,64]{1,0:T(8,128)S(1)} %get-tuple-element.201), channel_id=1, source_target_pairs={{1,0},{2,1},{3,2},{5,4},{6,5},{7,6},{9,8},{10,9},{11,10},{13,12},{... | collective-permute-start | bytes 30728 | tf_op jit(solution)/shard_map/ppermute | solution.py:27
  101.7 6.5 collective-permute-start.12
  103.7 11.5 collective-permute-start.13
  115.4 18.4 %copy-start.2 = (f32[40,1024]{1,0:T(8,128)}, f32[40,1024]{1,0:T(8,128)S(1)}, u32[]{:S(2)}) copy-start(f32[40,1024]{1,0:T(8,128)S(1)} %fusion.63) | copy-start | bytes 491524
  174.9 0.7 copy-start.4
  174.9 1427.0 %all-gather.2.cloned.1.call-start = ((), (), s32[]{:S(2)}) async-start(), calls=%async_computation.2 | async-start | bytes 2113536 | tf_op jit(solution)/shard_map/all_gather | solution.py:95
Sparse Core Ops, SparseCore 0:
  175.0 738.9 reduce-scatter.1
  916.7 685.1 all-gather.1
where the time goes:
time: 1640 us
  waiting for transfers between devices  1450 us (88%)
  starting transfers between devices  70.9 us (4%)
  matrix products  34.8 us (2%)
  local copies, waits for them, and re-layouts  30.8 us (2%)
  blocking collectives  18.1 us (1%)
    reduce_scatter x1, waiting for transfers between devices, body(): lax.psum_scatter(result.reshape(row_count, 2 * MODES), 'slab', scatter_di...  738 us
    all_gather x1, waiting for transfers between devices, body(): portion = lax.all_gather(filtered, 'slab', axis=0, tiled=True)  686 us
    ppermute x8, starting transfers between devices, extended_2(): after = lax.ppermute(leading, axis, down)  51.1 us
  transfers between devices with their start and end apart: 18, of which 6 were waited for; matrix products, arithmetic and copies ran while one was open for 0% of the time, Pallas kernels for 0%

commit v1 on v0

v1 whole, which is shorter than its diff:
```python
import functools
import math

import jax
import jax.numpy as jnp
import numpy as np
from jax import lax
from jax.experimental import pallas as pl
from jax.experimental.pallas import tpu as pltpu
from jax.sharding import PartitionSpec as P

COLS = 64
MODES = 64
WAVES = 4096
REGIONS = 8
STEPS = 4
PLANES = 5120
SLABS = 128
SECS = 4
DEPTH = PLANES // SLABS
HALO = STEPS
PADB = 64
K1 = WAVES // SLABS
MODES_HERE = MODES // SECS
PAIRS = MODES_HERE // 2

courant_sq = 0.14
two_pi = 2.0 * math.pi
HIGHEST = lax.Precision.HIGHEST


def make_tables():
    k2 = np.arange(SLABS)
    first = two_pi * (np.outer(k2, k2) % SLABS) / SLABS
    dft_a = np.concatenate([np.cos(first), -np.sin(first)], axis=0)
    b = np.arange(PADB)
    live = (b < DEPTH).astype(np.float64)
    phi = two_pi * np.outer(k2, b) / PLANES
    tw_cos = np.tile(np.cos(phi) * live, (1, 2))
    tw_sin = np.tile(np.sin(phi) * live, (1, 2))
    psi = two_pi * (np.outer(b, np.arange(K1)) % DEPTH) / DEPTH
    pair = np.eye(2)
    c = np.kron(pair, np.cos(psi) * live[:, None])
    s = np.kron(pair, np.sin(psi) * live[:, None])
    forward = np.block([[c, -s], [s, c]])
    inverse = np.block([[c.T, s.T], [-s.T, c.T]])
    return [t.astype(np.float32) for t in (dft_a, tw_cos, tw_sin, forward, inverse)]


TABLES = make_tables()


def lookup_stiffness(region_ids, material):
    values = courant_sq * material[0] * material[1]
    match = region_ids[:, None] == jnp.arange(REGIONS, dtype=jnp.int32)[None, :]
    return jnp.sum(jnp.where(match, values[None, :], jnp.zeros_like(values)[None, :]), axis=1)


def advance_kernel(cur_ref, prev_ref, stiff_ref, shapes_ref, out_ref, modal_ref):
    current = cur_ref[...]
    before = prev_ref[...]
    planes, cells = current.shape
    stiff = stiff_ref[0:1, :]
    column = lax.broadcasted_iota(jnp.int32, (1, cells), 1) % COLS
    not_first = column > 0
    not_last = column < COLS - 1
    for _ in range(STEPS):
        west = jnp.where(not_first, pltpu.roll(current, 1, 1), 0.0)
        east = jnp.where(not_last, pltpu.roll(current, cells - 1, 1), 0.0)
        above = pltpu.roll(current, COLS, 1)
        below = pltpu.roll(current, cells - COLS, 1)
        prior = pltpu.roll(current, 1, 0)
        later = pltpu.roll(current, planes - 1, 0)
        summed = prior + later + above + below + west + east
        current, before = (
            2.0 * current - before + stiff * (summed - 6.0 * current),
            current,
        )
    edge = HALO * COLS
    final = current[HALO : planes - HALO, edge : cells - edge]
    out_ref[...] = final
    modal_ref[:, :DEPTH] = lax.dot_general(
        shapes_ref[...], final, (((1,), (1,)), ((), ())),
        precision=HIGHEST, preferred_element_type=jnp.float32,
    )
    modal_ref[:, DEPTH:] = jnp.zeros((MODES, PADB - DEPTH), jnp.float32)


def filter_kernel(
    x_ref, lower_ref, upper_ref, pc_ref, ps_ref, dft_ref, twc_ref, tws_ref, fwd_ref, inv_ref, out_ref
):
    dot = functools.partial(jnp.dot, precision=HIGHEST, preferred_element_type=jnp.float32)
    twc = twc_ref[...]
    tws = tws_ref[...]
    lanes = 2 * PADB
    row = lax.broadcasted_iota(jnp.int32, (SLABS, 4 * K1), 0)
    lane = lax.broadcasted_iota(jnp.int32, (SLABS, 4 * K1), 1)
    wave = row + SLABS * (lane % K1)
    for t in range(PAIRS):
        both = dot(dft_ref[...], x_ref[:, t * lanes : (t + 1) * lanes])
        real, imag = both[:SLABS], both[SLABS:]
        twisted = jnp.concatenate(
            [real * twc + imag * tws, imag * twc - real * tws], axis=1
        )
        spectrum = dot(twisted, fwd_ref[...])
        in_band = (wave >= lower_ref[t : t + 1, :]) & (wave < upper_ref[t : t + 1, :])
        filtered = jnp.where(in_band, spectrum, 0.0)
        back = dot(filtered, inv_ref[...])
        terms = back[:, :lanes] * pc_ref[...] - back[:, lanes:] * ps_ref[...]
        out_ref[t : t + 1, :] = jnp.sum(terms, axis=0, keepdims=True)


def shift_pair(last, leading, axis, peers, wrap):
    up = [(i, (i + 1) % peers) for i in range(peers if wrap else peers - 1)]
    down = [(j, i) for i, j in up]
    return lax.ppermute(last, axis, up), lax.ppermute(leading, axis, down)


def body(displacement, earlier_field, region_ids, material, mode_shapes, band_edges):
    cells = displacement.shape[1]
    stiffness = lookup_stiffness(region_ids, material)
    pile = jnp.concatenate(
        [displacement, earlier_field, jnp.broadcast_to(stiffness[None, :], (8, cells))], axis=0
    )
    edge = HALO * COLS
    before, after = shift_pair(pile[:, cells - edge :], pile[:, :edge], "sec", SECS, False)
    wide = jnp.concatenate([before, pile, after], axis=1)
    cur = wide[:DEPTH]
    prev = wide[DEPTH : 2 * DEPTH]
    stiff = wide[2 * DEPTH :]
    last = jnp.concatenate([cur[DEPTH - HALO :], prev[DEPTH - HALO :]], axis=0)
    leading = jnp.concatenate([cur[:HALO], prev[:HALO]], axis=0)
    before, after = shift_pair(last, leading, "slab", SLABS, True)
    cur = jnp.concatenate([before[:HALO], cur, after[:HALO]], axis=0)
    prev = jnp.concatenate([before[HALO:], prev, after[HALO:]], axis=0)
    shapes_t = mode_shapes.T
    current, modal_part = pl.pallas_call(
        advance_kernel,
        out_shape=(
            jax.ShapeDtypeStruct((DEPTH, cells), jnp.float32),
            jax.ShapeDtypeStruct((MODES, PADB), jnp.float32),
        ),
    )(cur, prev, stiff, shapes_t)
    modal = lax.psum_scatter(modal_part, "sec", scatter_dimension=0, tiled=True)
    x = lax.all_gather(modal.reshape(1, MODES_HERE * PADB), "slab", axis=0, tiled=True)

    slab = lax.axis_index("slab")
    k2 = jnp.arange(SLABS, dtype=jnp.int32)[:, None]
    lane_b = jnp.arange(2 * PADB, dtype=jnp.int32)[None, :] % PADB
    angle = ((k2 * (slab * DEPTH + lane_b)) % PLANES).astype(jnp.float32) * (two_pi / PLANES)
    pc = jnp.cos(angle) * (2.0 / PLANES)
    ps = jnp.sin(angle) * (2.0 / PLANES)
    edges = lax.dynamic_slice_in_dim(
        band_edges, lax.axis_index("sec") * MODES_HERE, MODES_HERE, axis=1
    )
    edges = jnp.broadcast_to(
        edges.reshape(2, PAIRS, 1, 2, 1), (2, PAIRS, 2, 2, K1)
    ).reshape(2, PAIRS, 4 * K1)
    smooth = pl.pallas_call(
        filter_kernel,
        out_shape=jax.ShapeDtypeStruct((PAIRS, 2 * PADB), jnp.float32),
    )(x, edges[0], edges[1], pc, ps, *[jnp.asarray(t) for t in TABLES])
    smooth = lax.all_gather(smooth.reshape(MODES_HERE, PADB), "sec", axis=0, tiled=True)
    band_field = lax.dot_general(
        smooth[:, :DEPTH], shapes_t, (((0,), (0,)), ((), ())),
        precision=HIGHEST, preferred_element_type=jnp.float32,
    ).astype(jnp.bfloat16)
    return current, band_field


def solution(mesh):
    return jax.shard_map(
        body,
        mesh=mesh,
        in_specs=(P("slab", "sec"), P("slab", "sec"), P("sec"), P(), P("sec", None), P()),
        out_specs=(P("slab", "sec"), P("slab", "sec")),
        check_vma=False,
    )
```

time: 1640 us -> 479 us (0.29)
  the two profiles are of different devices: /device:TPU:32 before, /device:TPU:1 now
where the time goes in v1:
time: 479 us; the launch traced here: 478 us
  blocking collectives  377 us (79%)
  waiting for transfers between devices  42.2 us (9%)
  starting transfers between devices  25.9 us (5%)
  between operations  14.2 us (3%)
  Pallas kernels  8.92 us (2%)
  other arithmetic  4.93 us (1%)
    all_gather x1, blocking collectives, body(): lax.all_gather(modal.reshape(1, MODES_HERE * PADB), 'slab', axis=0, tiled...  311 us
    all_gather x1, blocking collectives, body(): lax.all_gather(smooth.reshape(MODES_HERE, PADB), 'sec', axis=0, tiled=True)  65.5 us
    reduce_scatter x1, waiting for transfers between devices, body(): modal = lax.psum_scatter(modal_part, 'sec', scatter_dimension=0, tiled=True)  26.5 us
    ppermute x4, starting transfers between devices, shift_pair(): return (lax.ppermute(last, axis, up), lax.ppermute(leading, axis, down))  25.9 us
    ppermute x4, waiting for transfers between devices, shift_pair(): return (lax.ppermute(last, axis, up), lax.ppermute(leading, axis, down))  15.7 us
  transfers between devices with their start and end apart: 5, of which 3 were waited for; matrix products, arithmetic and copies ran while one was open for 1% of the time, Pallas kernels for 0%

profile of v1, /device:TPU:1, one launch (start us, length us, event | category | flops | bytes accessed | tf_op | source)
XLA Modules:
  0.0 478.2 jit_solution(18219501579490130809)
XLA Ops:
  7.2 0.0 copy-start
  7.2 0.0 reduce-scatter.2.cloned.1.call-start
  7.2 0.8 multiply_bitcast_fusion
  8.0 0.8 select_reduce_fusion
  8.8 0.0 copy-start.1
  8.8 0.9 pad_maximum_fusion.5
  9.7 8.8 %collective-permute-start = (f32[88,256]{1,0:T(8,128)S(1)}, f32[88,256]{1,0:T(8,128)S(1)}, u32[]{:S(2)}, u32[]{:S(2)}) collective-permute-start(f32[88,256]{1,0:T(8,128)S(1)} %get-tuple-element.15), channel_id=1, source_target_pairs={{0,1},{1,2},{2,3},{4,5},{5,6},{6,7},{8,9},{9,10},{10,11},{12,13},{... | collective-permute-start | bytes 270344 | tf_op jit(solution)/shard_map/ppermute | solution.py:116
  18.5 1.9 collective-permute-start.1
  20.5 0.9 sine_multiply_fusion
  21.4 0.1 constant_dynamic-slice_fusion
  21.5 6.9 %collective-permute-done.1 = f32[88,256]{1,0:T(8,128)S(1)} collective-permute-done((f32[88,256]{1,0:T(8,128)S(1)}, f32[88,256]{1,0:T(8,128)S(1)}, u32[]{:S(2)}, u32[]{:S(2)}) %collective-permute-start.1) | collective-permute-done | bytes 90144 | tf_op jit(solution)/shard_map/ppermute | solution.py:116
  28.4 0.6 pad_maximum_fusion.7
  29.0 13.2 %collective-permute-start.3 = (f32[8,1536]{1,0:T(8,128)S(1)}, f32[8,1536]{1,0:T(8,128)S(1)}, u32[]{:S(2)}, u32[]{:S(2)}) collective-permute-start(f32[8,1536]{1,0:T(8,128)S(1)} %get-tuple-element.12), channel_id=1, source_target_pairs={{4,0},{8,4},{12,8},{16,12},{20,16},{24,20},{28,24},{32,28},{36,32}... | collective-permute-start | bytes 147464 | tf_op jit(solution)/shard_map/ppermute | solution.py:116
  42.2 1.9 collective-permute-start.2
  44.3 8.8 %collective-permute-done.2 = f32[8,1536]{1,0:T(8,128)S(1)} collective-permute-done((f32[8,1536]{1,0:T(8,128)S(1)}, f32[8,1536]{1,0:T(8,128)S(1)}, u32[]{:S(2)}, u32[]{:S(2)}) %collective-permute-start.2) | collective-permute-done | bytes 49184 | tf_op jit(solution)/shard_map/ppermute | solution.py:116
  53.1 0.9 pad_maximum_fusion.1
  54.0 3.2 shard_map.122
  57.2 0.0 reduce-scatter.2.cloned.1.call-update
  57.2 0.1 slice.84
  57.3 0.1 broadcast_in_dim.44
  57.4 0.7 broadcast_in_dim.45.lower_ref
  58.1 0.1 slice.86
  58.2 0.1 broadcast_in_dim.46
  58.2 0.7 broadcast_in_dim.47.upper_ref
  58.9 26.5 %reduce-scatter.2.cloned.1.call-done = f32[16,64]{1,0:T(8,128)} async-done(((f32[64,64]{1,0:T(8,128)}), f32[16,64]{1,0:T(8,128)}) %reduce-scatter.2.cloned.1.call-update) | async-done | bytes 4112 | tf_op jit(solution)/shard_map/reduce_scatter | solution.py:144
  85.4 0.8 reshape.46
  86.2 311.4 %all-gather = f32[128,1,1024]{2,1,0:T(1,128)S(1)} all-gather(f32[1,1,1024]{2,1,0:T(1,128)S(1)} %reshape.46), channel_id=1, replica_groups=mesh['slab'=128,'sec'=4] {'slab'}, dimensions={0}, use_global_device_ids=true | all-gather | bytes 528384 | tf_op jit(solution)/shard_map/all_gather | solution.py:145
  397.6 0.9 copy.15
  398.5 5.7 %shard_map.123 = f32[8,128]{1,0:T(8,128)} custom-call(f32[128,1024]{1,0:T(8,128)} %bitcast.7, s32[8,128]{1,0:T(8,128)} %broadcast_in_dim.45.lower_ref, s32[8,128]{1,0:T(8,128)} %broadcast_in_dim.47.upper_ref, f32[128,128]{1,0:T(8,128)} %get-tuple-element.22.pc_ref, f32[128,128]{1,0:T(8,128)} %get-tuple-element.21.ps_ref, f32[256,128]{1,0:T(8,128)} %constant.60.clone.dft_ref, ...), custom_call_target="tpu_custom_call" | custom-call | tf_op jit(solution)/shard_map/pallas_call | solution.py:159
  404.2 0.7 reshape.45
  404.9 65.5 %all_gather.7 = f32[64,64]{1,0:T(8,128)S(1)} all-gather(f32[16,64]{1,0:T(8,128)S(1)} %reshape.45), channel_id=1, replica_groups=mesh['slab'=128,'sec'=4] {'sec'}, dimensions={0}, use_global_device_ids=true | all-gather | bytes 20480 | tf_op jit(solution)/shard_map/all_gather | solution.py:163
  470.4 1.0 convolution_convert_fusion
  (16 shorter events, 0.2 us)
Async XLA Ops:
  7.2 14.2 %copy-start = (s32[2,64]{1,0:T(2,128)S(1)}, s32[2,64]{1,0:T(2,128)}, u32[]{:S(2)}) copy-start(s32[2,64]{1,0:T(2,128)} %param.16) | copy-start | bytes 1540
  7.2 78.2 %reduce-scatter.2.cloned.1.call-start = ((), (), s32[]{:S(2)}) async-start(), calls=%async_computation.1 | async-start | bytes 40960 | tf_op jit(solution)/shard_map/reduce_scatter | solution.py:144
  8.8 19.6 %copy-start.1 = (f32[40,1024]{1,0:T(8,128)S(1)}, f32[40,1024]{1,0:T(8,128)}, u32[]{:S(2)}) copy-start(f32[40,1024]{1,0:T(8,128)} %param.12) | copy-start | bytes 491524
  8.8 19.6 %copy-start.2 = (f32[40,1024]{1,0:T(8,128)S(1)}, f32[40,1024]{1,0:T(8,128)}, u32[]{:S(2)}) copy-start(f32[40,1024]{1,0:T(8,128)} %param.11) | copy-start | bytes 491524
  9.7 11.8 %collective-permute-start = (f32[88,256]{1,0:T(8,128)S(1)}, f32[88,256]{1,0:T(8,128)S(1)}, u32[]{:S(2)}, u32[]{:S(2)}) collective-permute-start(f32[88,256]{1,0:T(8,128)S(1)} %get-tuple-element.15), channel_id=1, source_target_pairs={{0,1},{1,2},{2,3},{4,5},{5,6},{6,7},{8,9},{9,10},{10,11},{12,13},{... | collective-permute-start | bytes 270344 | tf_op jit(solution)/shard_map/ppermute | solution.py:116
  18.5 9.9 %collective-permute-start.1 = (f32[88,256]{1,0:T(8,128)S(1)}, f32[88,256]{1,0:T(8,128)S(1)}, u32[]{:S(2)}, u32[]{:S(2)}) collective-permute-start(f32[88,256]{1,0:T(8,128)S(1)} %get-tuple-element.16), channel_id=1, source_target_pairs={{1,0},{2,1},{3,2},{5,4},{6,5},{7,6},{9,8},{10,9},{11,10},{13,12},{... | collective-permute-start | bytes 270344 | tf_op jit(solution)/shard_map/ppermute | solution.py:116
  29.0 15.2 %collective-permute-start.3 = (f32[8,1536]{1,0:T(8,128)S(1)}, f32[8,1536]{1,0:T(8,128)S(1)}, u32[]{:S(2)}, u32[]{:S(2)}) collective-permute-start(f32[8,1536]{1,0:T(8,128)S(1)} %get-tuple-element.12), channel_id=1, source_target_pairs={{4,0},{8,4},{12,8},{16,12},{20,16},{24,20},{28,24},{32,28},{36,32}... | collective-permute-start | bytes 147464 | tf_op jit(solution)/shard_map/ppermute | solution.py:116
  42.2 10.9 %collective-permute-start.2 = (f32[8,1536]{1,0:T(8,128)S(1)}, f32[8,1536]{1,0:T(8,128)S(1)}, u32[]{:S(2)}, u32[]{:S(2)}) collective-permute-start(f32[8,1536]{1,0:T(8,128)S(1)} %get-tuple-element.8), channel_id=1, source_target_pairs={{0,4},{4,8},{8,12},{12,16},{16,20},{20,24},{24,28},{28,32},{32,36}... | collective-permute-start | bytes 147464 | tf_op jit(solution)/shard_map/ppermute | solution.py:116
  398.5 71.9 %copy-start.3 = (f32[1024,64]{0,1:T(8,128)S(1)}, f32[1024,64]{0,1:T(8,128)}, u32[]{:S(2)}) copy-start(f32[1024,64]{0,1:T(8,128)} %param.15) | copy-start | bytes 786436
Sparse Core Ops, SparseCore 0:
  57.3 28.0 reduce-scatter.1

commit v2 on v1

--- a/solution.py
+++ b/solution.py
@@ -21,8 +21,10 @@
 HALO = STEPS
 PADB = 64
 K1 = WAVES // SLABS
-MODES_HERE = MODES // SECS
-PAIRS = MODES_HERE // 2
+ZS = 8
+PLACES = SLABS // ZS
+GROUP = ZS * SECS
+MESH = pl.DeviceIdType.MESH
 
 courant_sq = 0.14
 two_pi = 2.0 * math.pi
@@ -31,7 +33,8 @@
 
 def make_tables():
     k2 = np.arange(SLABS)
-    first = two_pi * (np.outer(k2, k2) % SLABS) / SLABS
+    held_a = (np.arange(ZS)[None, :] * PLACES + np.arange(PLACES)[:, None]).reshape(-1)
+    first = two_pi * (np.outer(k2, held_a) % SLABS) / SLABS
     dft_a = np.concatenate([np.cos(first), -np.sin(first)], axis=0)
     b = np.arange(PADB)
     live = (b < DEPTH).astype(np.float64)
@@ -87,27 +90,95 @@
 
 
 def filter_kernel(
-    x_ref, lower_ref, upper_ref, pc_ref, ps_ref, dft_ref, twc_ref, tws_ref, fwd_ref, inv_ref, out_ref
+    modal_ref, lower_ref, upper_ref, rows_ref, dft_ref, twc_ref, tws_ref, fwd_ref, inv_ref, out_ref,
+    pieces, mine, held, sent, send1, recv1, send2, recv2, send3, recv3,
 ):
+    slab = lax.axis_index("slab")
+    sec = lax.axis_index("sec")
+    z, place = slab // PLACES, slab % PLACES
+    group = z * SECS + sec
+
+    def in_group(step):
+        other = lax.rem(group + step, GROUP)
+        other_z = other // SECS
+        return other, other_z, {"slab": other_z * PLACES + place, "sec": lax.rem(other, SECS)}
+
+    def in_places(step):
+        return {"slab": z * PLACES + lax.rem(place + step, PLACES), "sec": sec}
+
+    barrier = pltpu.get_barrier_semaphore()
+
+    @pl.loop(1, GROUP)
+    def _(step):
+        pl.semaphore_signal(barrier, inc=1, device_id=in_group(step)[2], device_id_type=MESH)
+
+    @pl.loop(1, PLACES)
+    def _(step):
+        pl.semaphore_signal(barrier, inc=1, device_id=in_places(step), device_id_type=MESH)
+
+    pl.semaphore_wait(barrier, GROUP + PLACES - 2)
+
+    @pl.loop(1, GROUP)
+    def _(step):
+        other, _, device = in_group(step)
+        pltpu.make_async_remote_copy(
+            src_ref=modal_ref.at[other], dst_ref=pieces.at[group],
+            send_sem=send1, recv_sem=recv1, device_id=device, device_id_type=MESH,
+        ).start()
+
+    pltpu.make_async_copy(modal_ref.at[group], pieces.at[group], recv1).start()
+    pltpu.make_async_copy(pieces, pieces, recv1).wait()
+    for i in range(ZS):
+        total = pieces[SECS * i] + pieces[SECS * i + 1]
+        total = total + pieces[SECS * i + 2] + pieces[SECS * i + 3]
+        mine[i : i + 1, :] = total
+
+    @pl.loop(1, PLACES)
+    def _(step):
+        pltpu.make_async_remote_copy(
+            src_ref=mine, dst_ref=held.at[place],
+            send_sem=send2, recv_sem=recv2, device_id=in_places(step), device_id_type=MESH,
+        ).start()
+
+    pltpu.make_async_copy(mine, held.at[place], recv2).start()
+    pltpu.make_async_copy(held, held, recv2).wait()
+
     dot = functools.partial(jnp.dot, precision=HIGHEST, preferred_element_type=jnp.float32)
+    lanes = 2 * PADB
     twc = twc_ref[...]
     tws = tws_ref[...]
-    lanes = 2 * PADB
     row = lax.broadcasted_iota(jnp.int32, (SLABS, 4 * K1), 0)
     lane = lax.broadcasted_iota(jnp.int32, (SLABS, 4 * K1), 1)
     wave = row + SLABS * (lane % K1)
-    for t in range(PAIRS):
-        both = dot(dft_ref[...], x_ref[:, t * lanes : (t + 1) * lanes])
-        real, imag = both[:SLABS], both[SLABS:]
-        twisted = jnp.concatenate(
-            [real * twc + imag * tws, imag * twc - real * tws], axis=1
-        )
-        spectrum = dot(twisted, fwd_ref[...])
-        in_band = (wave >= lower_ref[t : t + 1, :]) & (wave < upper_ref[t : t + 1, :])
-        filtered = jnp.where(in_band, spectrum, 0.0)
-        back = dot(filtered, inv_ref[...])
-        terms = back[:, :lanes] * pc_ref[...] - back[:, lanes:] * ps_ref[...]
-        out_ref[t : t + 1, :] = jnp.sum(terms, axis=0, keepdims=True)
+    both = dot(dft_ref[...], held[...].reshape(SLABS, lanes))
+    real, imag = both[:SLABS], both[SLABS:]
+    twisted = jnp.concatenate([real * twc + imag * tws, imag * twc - real * tws], axis=1)
+    spectrum = dot(twisted, fwd_ref[...])
+    in_band = (wave >= lower_ref[...]) & (wave < upper_ref[...])
+    filtered = jnp.where(in_band, spectrum, 0.0)
+    back = dot(filtered, inv_ref[...])
+    real, imag = back[:, :lanes], back[:, lanes:]
+    twisted = jnp.concatenate([real * twc - imag * tws, imag * twc + real * tws], axis=0)
+    smooth = dot(rows_ref[...], twisted)
+    for i in range(ZS):
+        sent[i] = smooth[i : i + 1, :]
+
+    @pl.loop(1, GROUP)
+    def _(step):
+        _, other_z, device = in_group(step)
+        pltpu.make_async_remote_copy(
+            src_ref=sent.at[other_z], dst_ref=out_ref.at[group],
+            send_sem=send3, recv_sem=recv3, device_id=device, device_id_type=MESH,
+        ).start()
+
+    pltpu.make_async_copy(sent.at[z], out_ref.at[group], recv3).start()
+    pltpu.make_async_copy(out_ref, out_ref, recv3).wait()
+    most = pieces.at[pl.ds(0, GROUP - 1)]
+    pltpu.make_async_copy(most, most, send1).wait()
+    most = held.at[pl.ds(0, PLACES - 1)]
+    pltpu.make_async_copy(most, most, send2).wait()
+    most = out_ref.at[pl.ds(0, GROUP - 1)]
+    pltpu.make_async_copy(most, most, send3).wait()
 
 
 def shift_pair(last, leading, axis, peers, wrap):
@@ -141,26 +212,33 @@
             jax.ShapeDtypeStruct((MODES, PADB), jnp.float32),
         ),
     )(cur, prev, stiff, shapes_t)
-    modal = lax.psum_scatter(modal_part, "sec", scatter_dimension=0, tiled=True)
-    x = lax.all_gather(modal.reshape(1, MODES_HERE * PADB), "slab", axis=0, tiled=True)
-
     slab = lax.axis_index("slab")
-    k2 = jnp.arange(SLABS, dtype=jnp.int32)[:, None]
-    lane_b = jnp.arange(2 * PADB, dtype=jnp.int32)[None, :] % PADB
-    angle = ((k2 * (slab * DEPTH + lane_b)) % PLANES).astype(jnp.float32) * (two_pi / PLANES)
-    pc = jnp.cos(angle) * (2.0 / PLANES)
-    ps = jnp.sin(angle) * (2.0 / PLANES)
-    edges = lax.dynamic_slice_in_dim(
-        band_edges, lax.axis_index("sec") * MODES_HERE, MODES_HERE, axis=1
-    )
-    edges = jnp.broadcast_to(
-        edges.reshape(2, PAIRS, 1, 2, 1), (2, PAIRS, 2, 2, K1)
-    ).reshape(2, PAIRS, 4 * K1)
+    group = slab // PLACES * SECS + lax.axis_index("sec")
+    k2 = jnp.arange(SLABS, dtype=jnp.int32)[None, :]
+    places = jnp.arange(ZS, dtype=jnp.int32)[:, None] * PLACES + slab % PLACES
+    angle = ((k2 * places) % SLABS).astype(jnp.float32) * (two_pi / SLABS)
+    rows = jnp.concatenate([jnp.cos(angle), -jnp.sin(angle)], axis=1) * (2.0 / PLANES)
+    edges = lax.dynamic_slice_in_dim(band_edges, group * 2, 2, axis=1)
+    edges = jnp.broadcast_to(edges.reshape(2, 1, 2, 1), (2, 2, 2, K1)).reshape(2, 4 * K1)
+    dma = pltpu.SemaphoreType.DMA
     smooth = pl.pallas_call(
         filter_kernel,
-        out_shape=jax.ShapeDtypeStruct((PAIRS, 2 * PADB), jnp.float32),
-    )(x, edges[0], edges[1], pc, ps, *[jnp.asarray(t) for t in TABLES])
-    smooth = lax.all_gather(smooth.reshape(MODES_HERE, PADB), "sec", axis=0, tiled=True)
+        out_shape=jax.ShapeDtypeStruct((GROUP, 1, 2 * PADB), jnp.float32),
+        in_specs=[pl.BlockSpec(memory_space=pltpu.VMEM)] * 9,
+        out_specs=pl.BlockSpec(memory_space=pltpu.VMEM),
+        scratch_shapes=[
+            pltpu.VMEM((GROUP, 1, 2 * PADB), jnp.float32),
+            pltpu.VMEM((ZS, 2 * PADB), jnp.float32),
+            pltpu.VMEM((PLACES, ZS, 2 * PADB), jnp.float32),
+            pltpu.VMEM((ZS, 1, 2 * PADB), jnp.float32),
+            dma, dma, dma, dma, dma, dma,
+        ],
+        compiler_params=pltpu.CompilerParams(collective_id=0, has_side_effects=True),
+    )(
+        modal_part.reshape(GROUP, 1, 2 * PADB), edges[0:1], edges[1:2], rows,
+        *[jnp.asarray(t) for t in TABLES],
+    )
+    smooth = smooth.reshape(MODES, PADB)
     band_field = lax.dot_general(
         smooth[:, :DEPTH], shapes_t, (((0,), (0,)), ((), ())),
         precision=HIGHEST, preferred_element_type=jnp.float32,

time: 479 us -> 81.1 us (0.17)
  blocking collectives: 377 us -> 0 us
  waiting for transfers between devices: 42.2 us -> 14.4 us
  Pallas kernels: 8.92 us -> 28.3 us
  between operations: 14.2 us -> 0.79 us
    all_gather x2 -> x0, blocking collectives: 377 us -> none  [the longest x1 311 us: body(): lax.all_gather(modal.reshape(1, MODES_HERE * PADB), 'slab', axis=0, tiled...]
    reduce_scatter x1 -> x0, waiting for transfers between devices: 26.5 us -> none  [body(): modal = lax.psum_scatter(modal_part, 'sec', scatter_dimension=0, tiled=True)]
    pallas_call x1, Pallas kernels: 5.72 us -> 25.2 us  [body(): pl.pallas_call(filter_kernel, out_shape=jax.ShapeDtypeStruct((GROUP, 1, 2...]
  transfers between devices with their start and end apart: 5 -> 4, of which waited for: 3 -> 2; matrix products, arithmetic and copies ran while one was open for 1% -> 3% of each run, Pallas kernels for 0% -> 0%
where the time goes in v2:
time: 81.1 us; the launch traced here: 80.6 us
  Pallas kernels  28.3 us (35%)
  starting transfers between devices  26.4 us (33%)
  waiting for transfers between devices  14.4 us (18%)
  other arithmetic  6.14 us (8%)
  local copies, waits for them, and re-layouts  3.6 us (4%)
  matrix products  0.98 us (1%)
    ppermute x4, starting transfers between devices, shift_pair(): return (lax.ppermute(last, axis, up), lax.ppermute(leading, axis, down))  26.4 us
    pallas_call x1, Pallas kernels, body(): pl.pallas_call(filter_kernel, out_shape=jax.ShapeDtypeStruct((GROUP, 1, 2...  25.2 us
    ppermute x4, waiting for transfers between devices, shift_pair(): return (lax.ppermute(last, axis, up), lax.ppermute(leading, axis, down))  14.4 us
    pallas_call x1, Pallas kernels, body(): pl.pallas_call(advance_kernel, out_shape=(jax.ShapeDtypeStruct((DEPTH, ce...  3.2 us
  transfers between devices with their start and end apart: 4, of which 2 were waited for; matrix products, arithmetic and copies ran while one was open for 3% of the time, Pallas kernels for 0%

profile of v2, /device:TPU:1, one launch (start us, length us, event | category | flops | bytes accessed | tf_op | source)
XLA Modules:
  0.0 80.6 jit_solution(9431139727438277633)
XLA Ops:
  0.6 0.0 copy-start
  0.6 0.8 multiply_bitcast_fusion
  1.4 0.8 select_reduce_fusion
  2.2 0.0 copy-start.1
  2.2 0.0 copy-start.2
  2.2 0.9 %pad_maximum_fusion.5 = (f32[88,256]{1,0:T(8,128)S(1)}, f32[88,256]{1,0:T(8,128)S(1)}) fusion(f32[8,1024]{1,0:T(8,128)S(1)} %broadcast_in_dim.43, f32[40,1024]{1,0:T(8,128)} %param.12, f32[40,1024]{1,0:T(8,128)} %param.11), kind=kLoop, calls=%fused_computation.6 | loop fusion | flops 90112 | bytes 540672 | tf_op jit(solution)/shard_map/slice | solution.py:197
  3.1 8.8 %collective-permute-start = (f32[88,256]{1,0:T(8,128)S(1)}, f32[88,256]{1,0:T(8,128)S(1)}, u32[]{:S(2)}, u32[]{:S(2)}) collective-permute-start(f32[88,256]{1,0:T(8,128)S(1)} %get-tuple-element.13), channel_id=1, source_target_pairs={{0,1},{1,2},{2,3},{4,5},{5,6},{6,7},{8,9},{9,10},{10,11},{12,13},{... | collective-permute-start | bytes 270344 | tf_op jit(solution)/shard_map/ppermute | solution.py:187
  12.0 1.9 %collective-permute-start.1 = (f32[88,256]{1,0:T(8,128)S(1)}, f32[88,256]{1,0:T(8,128)S(1)}, u32[]{:S(2)}, u32[]{:S(2)}) collective-permute-start(f32[88,256]{1,0:T(8,128)S(1)} %get-tuple-element.14), channel_id=1, source_target_pairs={{1,0},{2,1},{3,2},{5,4},{6,5},{7,6},{9,8},{10,9},{11,10},{13,12},{... | collective-permute-start | bytes 270344 | tf_op jit(solution)/shard_map/ppermute | solution.py:187
  13.9 0.0 copy-done
  13.9 0.1 constant_dynamic-slice_fusion
  14.0 0.1 broadcast_in_dim.44
  14.1 0.6 broadcast_in_dim.45.lower_ref
  14.7 0.1 broadcast_in_dim.46
  14.8 0.7 broadcast_in_dim.47.upper_ref
  15.4 0.1 fusion.20
  15.5 0.6 maximum_multiply_fusion.rows_ref
  16.1 0.0 collective-permute-done
  16.1 5.6 %collective-permute-done.1 = f32[88,256]{1,0:T(8,128)S(1)} collective-permute-done((f32[88,256]{1,0:T(8,128)S(1)}, f32[88,256]{1,0:T(8,128)S(1)}, u32[]{:S(2)}, u32[]{:S(2)}) %collective-permute-start.1) | collective-permute-done | bytes 90144 | tf_op jit(solution)/shard_map/ppermute | solution.py:187
  21.7 0.0 copy-done.1
  21.7 0.6 pad_maximum_fusion.7
  22.4 13.7 %collective-permute-start.3 = (f32[8,1536]{1,0:T(8,128)S(1)}, f32[8,1536]{1,0:T(8,128)S(1)}, u32[]{:S(2)}, u32[]{:S(2)}) collective-permute-start(f32[8,1536]{1,0:T(8,128)S(1)} %get-tuple-element.10), channel_id=1, source_target_pairs={{4,0},{8,4},{12,8},{16,12},{20,16},{24,20},{28,24},{32,28},{36,32}... | collective-permute-start | bytes 147464 | tf_op jit(solution)/shard_map/ppermute | solution.py:187
  36.1 1.9 %collective-permute-start.2 = (f32[8,1536]{1,0:T(8,128)S(1)}, f32[8,1536]{1,0:T(8,128)S(1)}, u32[]{:S(2)}, u32[]{:S(2)}) collective-permute-start(f32[8,1536]{1,0:T(8,128)S(1)} %get-tuple-element.6), channel_id=1, source_target_pairs={{0,4},{4,8},{8,12},{12,16},{16,20},{20,24},{24,28},{28,32},{32,36}... | collective-permute-start | bytes 147464 | tf_op jit(solution)/shard_map/ppermute | solution.py:187
  38.1 0.0 collective-permute-done.3
  38.1 8.8 %collective-permute-done.2 = f32[8,1536]{1,0:T(8,128)S(1)} collective-permute-done((f32[8,1536]{1,0:T(8,128)S(1)}, f32[8,1536]{1,0:T(8,128)S(1)}, u32[]{:S(2)}, u32[]{:S(2)}) %collective-permute-start.2) | collective-permute-done | bytes 49184 | tf_op jit(solution)/shard_map/ppermute | solution.py:187
  47.0 0.9 %pad_maximum_fusion.1 = (f32[48,1536]{1,0:T(8,128)}, f32[48,1536]{1,0:T(8,128)}) fusion(f32[4,1536]{1,0:T(4,128)S(1)} %get-tuple-element.18, f32[40,1536]{1,0:T(8,128)S(1)} %get-tuple-element.12, f32[4,1536]{1,0:T(4,128)S(1)} %get-tuple-element.16, f32[4,1536]{1,0:T(4,128)S(1)} %get-tuple-element.17, f32[40,1536]{1,0:T(8,128)S(1)} %get-tuple-element.11, ...), kind=kLoop, calls=%fused_computation.2 | loop fusion | flops 294912 | bytes 1179648 | tf_op jit(solution)/shard_map/concatenate | solution.py:205
  47.9 3.2 %shard_map.122 = (f32[40,1024]{1,0:T(8,128)}, f32[64,64]{1,0:T(8,128)}) custom-call(f32[48,1536]{1,0:T(8,128)} %get-tuple-element.23.cur_ref, f32[48,1536]{1,0:T(8,128)} %get-tuple-element.24.prev_ref, f32[8,1536]{1,0:T(8,128)} %get-tuple-element.9.stiff_ref, f32[64,1024]{1,0:T(8,128)} %bitcast.8), custom_call_target="tpu_custom_call" | custom-call | tf_op jit(solution)/shard_map/pallas_call | solution.py:208
  51.1 1.4 %reshape.32.modal_ref = f32[32,1,128]{2,1,0:T(1,128)} reshape(f32[64,64]{1,0:T(8,128)} %get-tuple-element.5) | data formatting | bytes 32768 | tf_op jit(solution)/shard_map/reshape | solution.py:238
  52.5 25.2 %shard_map.123 = f32[32,1,128]{2,1,0:T(1,128)} custom-call(f32[32,1,128]{2,1,0:T(1,128)} %reshape.32.modal_ref, s32[1,128]{1,0:T(1,128)} %broadcast_in_dim.45.lower_ref, s32[1,128]{1,0:T(1,128)} %broadcast_in_dim.47.upper_ref, f32[8,256]{1,0:T(8,128)} %maximum_multiply_fusion.rows_ref, f32[256,128]{1,0:T(8,128)} %constant.75.clone.dft_ref, ...), custom_call_target="tpu_custom_call" | custom-call | tf_op jit(solution)/shard_map/pallas_call | solution.py:224
  77.7 0.5 broadcast.89
  78.2 1.4 %reduce.3 = f32[32,128]{1,0:T(8,128)S(1)} reduce(f32[32,1,128]{2,1,0:T(1,128)} %shard_map.123, f32[]{:T(128)} %broadcast.89), dimensions={1}, to_apply=%pallas_call.11.reduce_sub_computation.3 | reduce | bytes 32772 | tf_op jit(solution)/shard_map/pallas_call | solution.py:224
  79.6 0.1 reshape.33
  79.7 1.0 %convolution_convert_fusion = bf16[40,1024]{1,0:T(8,128)(2,1)} fusion(f32[1024,64]{0,1:T(8,128)S(1)} %copy-done.3, f32[64,64]{1,0:T(8,128)S(1)} %reshape.33), kind=kOutput, calls=%fused_computation | convolution fusion | flops 31498240 | bytes 360448 | tf_op jit(solution)/shard_map/dot_general | solution.py:242
  (11 shorter events, 0.1 us)
Async XLA Ops:
  0.6 13.3 %copy-start = (s32[2,64]{1,0:T(2,128)S(1)}, s32[2,64]{1,0:T(2,128)}, u32[]{:S(2)}) copy-start(s32[2,64]{1,0:T(2,128)} %param.16) | copy-start | bytes 1540
  2.2 19.5 %copy-start.1 = (f32[40,1024]{1,0:T(8,128)S(1)}, f32[40,1024]{1,0:T(8,128)}, u32[]{:S(2)}) copy-start(f32[40,1024]{1,0:T(8,128)} %param.12) | copy-start | bytes 491524
  2.2 19.5 %copy-start.2 = (f32[40,1024]{1,0:T(8,128)S(1)}, f32[40,1024]{1,0:T(8,128)}, u32[]{:S(2)}) copy-start(f32[40,1024]{1,0:T(8,128)} %param.11) | copy-start | bytes 491524
  3.1 13.0 %collective-permute-start = (f32[88,256]{1,0:T(8,128)S(1)}, f32[88,256]{1,0:T(8,128)S(1)}, u32[]{:S(2)}, u32[]{:S(2)}) collective-permute-start(f32[88,256]{1,0:T(8,128)S(1)} %get-tuple-element.13), channel_id=1, source_target_pairs={{0,1},{1,2},{2,3},{4,5},{5,6},{6,7},{8,9},{9,10},{10,11},{12,13},{... | collective-permute-start | bytes 270344 | tf_op jit(solution)/shard_map/ppermute | solution.py:187
  12.0 9.8 %collective-permute-start.1 = (f32[88,256]{1,0:T(8,128)S(1)}, f32[88,256]{1,0:T(8,128)S(1)}, u32[]{:S(2)}, u32[]{:S(2)}) collective-permute-start(f32[88,256]{1,0:T(8,128)S(1)} %get-tuple-element.14), channel_id=1, source_target_pairs={{1,0},{2,1},{3,2},{5,4},{6,5},{7,6},{9,8},{10,9},{11,10},{13,12},{... | collective-permute-start | bytes 270344 | tf_op jit(solution)/shard_map/ppermute | solution.py:187
  22.4 15.7 %collective-permute-start.3 = (f32[8,1536]{1,0:T(8,128)S(1)}, f32[8,1536]{1,0:T(8,128)S(1)}, u32[]{:S(2)}, u32[]{:S(2)}) collective-permute-start(f32[8,1536]{1,0:T(8,128)S(1)} %get-tuple-element.10), channel_id=1, source_target_pairs={{4,0},{8,4},{12,8},{16,12},{20,16},{24,20},{28,24},{32,28},{36,32}... | collective-permute-start | bytes 147464 | tf_op jit(solution)/shard_map/ppermute | solution.py:187
  36.1 10.9 %collective-permute-start.2 = (f32[8,1536]{1,0:T(8,128)S(1)}, f32[8,1536]{1,0:T(8,128)S(1)}, u32[]{:S(2)}, u32[]{:S(2)}) collective-permute-start(f32[8,1536]{1,0:T(8,128)S(1)} %get-tuple-element.6), channel_id=1, source_target_pairs={{0,4},{4,8},{8,12},{12,16},{16,20},{20,24},{24,28},{28,32},{32,36}... | collective-permute-start | bytes 147464 | tf_op jit(solution)/shard_map/ppermute | solution.py:187
  52.5 27.2 %copy-start.3 = (f32[1024,64]{0,1:T(8,128)S(1)}, f32[1024,64]{0,1:T(8,128)}, u32[]{:S(2)}) copy-start(f32[1024,64]{0,1:T(8,128)} %param.15) | copy-start | bytes 786436

commit v3 on v2

v3 whole, which is shorter than its diff:
```python
import functools
import math

import jax
import jax.numpy as jnp
import numpy as np
from jax import lax
from jax.experimental import pallas as pl
from jax.experimental.pallas import tpu as pltpu
from jax.sharding import PartitionSpec as P

COLS = 64
MODES = 64
WAVES = 4096
REGIONS = 8
STEPS = 4
PLANES = 5120
SLABS = 128
SECS = 4
DEPTH = PLANES // SLABS
PAD = 8
EDGE = STEPS * COLS
CELLS_HERE = 4096 // SECS
TALL = DEPTH + 2 * PAD
BROAD = CELLS_HERE + 2 * EDGE
BESIDE = ((0, 1), (0, -1), (1, 0), (-1, 0), (1, 1), (1, -1), (-1, 1), (-1, -1))
PADB = 64
K1 = WAVES // SLABS
ZS = 8
PLACES = SLABS // ZS
GROUP = ZS * SECS
MESH = pl.DeviceIdType.MESH

courant_sq = 0.14
two_pi = 2.0 * math.pi
HIGHEST = lax.Precision.HIGHEST


def make_tables():
    k2 = np.arange(SLABS)
    held_a = (np.arange(ZS)[None, :] * PLACES + np.arange(PLACES)[:, None]).reshape(-1)
    first = two_pi * (np.outer(k2, held_a) % SLABS) / SLABS
    dft_a = np.concatenate([np.cos(first), -np.sin(first)], axis=0)
    b = np.arange(PADB)
    live = (b < DEPTH).astype(np.float64)
    phi = two_pi * np.outer(k2, b) / PLANES
    tw_cos = np.tile(np.cos(phi) * live, (1, 2))
    tw_sin = np.tile(np.sin(phi) * live, (1, 2))
    psi = two_pi * (np.outer(b, np.arange(K1)) % DEPTH) / DEPTH
    pair = np.eye(2)
    c = np.kron(pair, np.cos(psi) * live[:, None])
    s = np.kron(pair, np.sin(psi) * live[:, None])
    forward = np.block([[c, -s], [s, c]])
    inverse = np.block([[c.T, s.T], [-s.T, c.T]])
    at = held_a.reshape(PLACES, ZS, 1) * k2
    last = two_pi * (at % SLABS) / SLABS
    rows = np.concatenate([np.cos(last), -np.sin(last)], axis=2) * (2.0 / PLANES)
    return [t.astype(np.float32) for t in (rows, dft_a, tw_cos, tw_sin, forward, inverse)]


TABLES = make_tables()


def rail_kernel(
    disp_ref, earlier_ref, region_ref, material_ref, edges_ref, shapes_ref,
    rows_ref, dft_ref, twc_ref, tws_ref, fwd_ref, inv_ref,
    out_ref, band_ref,
    stiff_ref, wide, modal_ref, pieces, mine, held, sent, smooth_ref,
    send0, recv0, send1, recv1, send2, recv2, send3, recv3,
):
    slab = lax.axis_index("slab")
    sec = lax.axis_index("sec")
    z, place = slab // PLACES, slab % PLACES
    group = z * SECS + sec

    def in_group(step):
        other = lax.rem(group + step, GROUP)
        other_z = other // SECS
        return other, other_z, {"slab": other_z * PLACES + place, "sec": lax.rem(other, SECS)}

    def in_places(step):
        return {"slab": z * PLACES + lax.rem(place + step, PLACES), "sec": sec}

    def beside(up, across):
        return {
            "slab": lax.rem(slab + (SLABS + up), SLABS),
            "sec": lax.rem(sec + (SECS + across), SECS),
        }

    barrier = pltpu.get_barrier_semaphore()

    @pl.loop(1, GROUP)
    def _(step):
        pl.semaphore_signal(barrier, inc=1, device_id=in_group(step)[2], device_id_type=MESH)

    @pl.loop(1, PLACES)
    def _(step):
        pl.semaphore_signal(barrier, inc=1, device_id=in_places(step), device_id_type=MESH)

    for up, across in BESIDE:
        pl.semaphore_signal(barrier, inc=1, device_id=beside(up, across), device_id_type=MESH)

    stiff = jnp.zeros((8, CELLS_HERE), jnp.float32)
    region = jnp.broadcast_to(region_ref[...], (8, CELLS_HERE))
    for r in range(REGIONS):
        value = courant_sq * material_ref[0, r] * material_ref[1, r]
        stiff = jnp.where(region == r, value, stiff)
    stiff_ref[...] = stiff

    pl.semaphore_wait(barrier, GROUP + PLACES - 2 + len(BESIDE))

    halo_copies = []

    def send_halo(src, base, src_rows, dst_rows, up, across):
        src_at, dst_at = {-1: (0, EDGE + CELLS_HERE), 1: (CELLS_HERE - EDGE, 0), 0: (0, EDGE)}[across]
        count = CELLS_HERE if across == 0 else EDGE
        src = src.at[pl.ds(*src_rows), pl.ds(src_at, count)]
        dst = wide.at[pl.ds(base + dst_rows, src_rows[1]), pl.ds(dst_at, count)]
        if up == 0 and across == 0:
            pltpu.make_async_copy(src, dst, recv0).start()
            return
        copy = pltpu.make_async_remote_copy(
            src_ref=src, dst_ref=dst, send_sem=send0.at[len(halo_copies)], recv_sem=recv0,
            device_id=beside(up, across), device_id_type=MESH,
        )
        copy.start()
        halo_copies.append(copy)

    for up, across in BESIDE + ((0, 0),):
        src_rows, dst_rows = {
            -1: ((0, PAD), PAD + DEPTH), 1: ((DEPTH - PAD, PAD), 0), 0: ((0, DEPTH), PAD)
        }[up]
        send_halo(disp_ref, 0, src_rows, dst_rows, up, across)
        send_halo(earlier_ref, TALL, src_rows, dst_rows, up, across)
        if up == 0:
            send_halo(stiff_ref, 2 * TALL, (0, PAD), 0, up, across)
    pltpu.make_async_copy(wide, wide, recv0).wait()

    lane = lax.broadcasted_iota(jnp.int32, (1, BROAD), 1)
    start = jnp.where(sec == 0, EDGE, 0)
    stop = jnp.where(sec == SECS - 1, EDGE + CELLS_HERE, BROAD)
    inside = (lane >= start) & (lane < stop)
    current = jnp.where(inside, wide[:TALL, :], 0.0)
    before = jnp.where(inside, wide[TALL : 2 * TALL, :], 0.0)
    stiff = jnp.where(inside, wide[2 * TALL : 2 * TALL + 1, :], 0.0)
    not_first = lane % COLS > 0
    not_last = lane % COLS < COLS - 1
    for _ in range(STEPS):
        west = jnp.where(not_first, pltpu.roll(current, 1, 1), 0.0)
        east = jnp.where(not_last, pltpu.roll(current, BROAD - 1, 1), 0.0)
        above = pltpu.roll(current, COLS, 1)
        below = pltpu.roll(current, BROAD - COLS, 1)
        prior = pltpu.roll(current, 1, 0)
        later = pltpu.roll(current, TALL - 1, 0)
        summed = prior + later + above + below + west + east
        current, before = (
            2.0 * current - before + stiff * (summed - 6.0 * current),
            current,
        )
    final = current[PAD : PAD + DEPTH, EDGE : EDGE + CELLS_HERE]
    out_ref[...] = final
    lanes = 2 * PADB
    front = shapes_ref[:GROUP, :]
    back_half = shapes_ref[GROUP:, :]

    def dot_rows(shapes, planes):
        return lax.dot_general(
            shapes, planes, (((1,), (1,)), ((), ())),
            precision=HIGHEST, preferred_element_type=jnp.float32,
        )

    def blank(count):
        return jnp.zeros((count, CELLS_HERE), jnp.float32)

    modal = dot_rows(front, jnp.concatenate([final, blank(lanes - DEPTH)], axis=0))
    modal = modal + dot_rows(
        back_half, jnp.concatenate([blank(PADB), final, blank(PADB - DEPTH)], axis=0)
    )
    for i in range(GROUP):
        modal_ref[i] = modal[i : i + 1, :]

    @pl.loop(1, GROUP)
    def _(step):
        other, _, device = in_group(step)
        pltpu.make_async_remote_copy(
            src_ref=modal_ref.at[other], dst_ref=pieces.at[group],
            send_sem=send1, recv_sem=recv1, device_id=device, device_id_type=MESH,
        ).start()

    pltpu.make_async_copy(modal_ref.at[group], pieces.at[group], recv1).start()
    pltpu.make_async_copy(pieces, pieces, recv1).wait()
    for i in range(ZS):
        total = pieces[SECS * i] + pieces[SECS * i + 1]
        total = total + pieces[SECS * i + 2] + pieces[SECS * i + 3]
        mine[i : i + 1, :] = total

    @pl.loop(1, PLACES)
    def _(step):
        pltpu.make_async_remote_copy(
            src_ref=mine, dst_ref=held.at[place],
            send_sem=send2, recv_sem=recv2, device_id=in_places(step), device_id_type=MESH,
        ).start()

    pltpu.make_async_copy(mine, held.at[place], recv2).start()
    pltpu.make_async_copy(held, held, recv2).wait()

    dot = functools.partial(jnp.dot, precision=HIGHEST, preferred_element_type=jnp.float32)
    twc = twc_ref[...]
    tws = tws_ref[...]
    row = lax.broadcasted_iota(jnp.int32, (SLABS, 4 * K1), 0)
    lane = lax.broadcasted_iota(jnp.int32, (SLABS, 4 * K1), 1)
    wave = row + SLABS * (lane % K1)
    is_front = lane % (2 * K1) < K1
    lower = jnp.where(is_front, edges_ref[0, group], edges_ref[0, group + GROUP])
    upper = jnp.where(is_front, edges_ref[1, group], edges_ref[1, group + GROUP])
    both = dot(dft_ref[...], held[...].reshape(SLABS, lanes))
    real, imag = both[:SLABS], both[SLABS:]
    twisted = jnp.concatenate([real * twc + imag * tws, imag * twc - real * tws], axis=1)
    spectrum = dot(twisted, fwd_ref[...])
    in_band = (wave >= lower) & (wave < upper)
    filtered = jnp.where(in_band, spectrum, 0.0)
    back = dot(filtered, inv_ref[...])
    real, imag = back[:, :lanes], back[:, lanes:]
    twisted = jnp.concatenate([real * twc - imag * tws, imag * twc + real * tws], axis=0)
    smooth = dot(rows_ref[place], twisted)
    for i in range(ZS):
        sent[i] = smooth[i : i + 1, :]

    @pl.loop(1, GROUP)
    def _(step):
        _, other_z, device = in_group(step)
        pltpu.make_async_remote_copy(
            src_ref=sent.at[other_z], dst_ref=smooth_ref.at[group],
            send_sem=send3, recv_sem=recv3, device_id=device, device_id_type=MESH,
        ).start()

    pltpu.make_async_copy(sent.at[z], smooth_ref.at[group], recv3).start()
    pltpu.make_async_copy(smooth_ref, smooth_ref, recv3).wait()
    gathered = smooth_ref[:, 0, :].T
    band = dot(gathered[:DEPTH], front) + dot(gathered[PADB : PADB + DEPTH], back_half)
    band_ref[...] = band.astype(jnp.bfloat16)
    for copy in halo_copies:
        copy.wait_send()
    most = pieces.at[pl.ds(0, GROUP - 1)]
    pltpu.make_async_copy(most, most, send1).wait()
    most = held.at[pl.ds(0, PLACES - 1)]
    pltpu.make_async_copy(most, most, send2).wait()
    most = smooth_ref.at[pl.ds(0, GROUP - 1)]
    pltpu.make_async_copy(most, most, send3).wait()


def body(displacement, earlier_field, region_ids, material, mode_shapes, band_edges):
    vmem = pl.BlockSpec(memory_space=pltpu.VMEM)
    smem = pl.BlockSpec(memory_space=pltpu.SMEM)
    dma = pltpu.SemaphoreType.DMA
    lanes = 2 * PADB
    return pl.pallas_call(
        rail_kernel,
        out_shape=(
            jax.ShapeDtypeStruct((DEPTH, CELLS_HERE), jnp.float32),
            jax.ShapeDtypeStruct((DEPTH, CELLS_HERE), jnp.bfloat16),
        ),
        in_specs=[vmem] * 3 + [smem] * 2 + [vmem] * 7,
        out_specs=(vmem, vmem),
        scratch_shapes=[
            pltpu.VMEM((PAD, CELLS_HERE), jnp.float32),
            pltpu.VMEM((2 * TALL + PAD, BROAD), jnp.float32),
            pltpu.VMEM((GROUP, 1, lanes), jnp.float32),
            pltpu.VMEM((GROUP, 1, lanes), jnp.float32),
            pltpu.VMEM((ZS, lanes), jnp.float32),
            pltpu.VMEM((PLACES, ZS, lanes), jnp.float32),
            pltpu.VMEM((ZS, 1, lanes), jnp.float32),
            pltpu.VMEM((GROUP, 1, lanes), jnp.float32),
            dma((18,)), dma, dma, dma, dma, dma, dma, dma,
        ],
        compiler_params=pltpu.CompilerParams(collective_id=0, has_side_effects=True),
    )(
        displacement, earlier_field, region_ids.reshape(1, CELLS_HERE), material, band_edges,
        mode_shapes.T, *[jnp.asarray(t) for t in TABLES],
    )


def solution(mesh):
    return jax.shard_map(
        body,
        mesh=mesh,
        in_specs=(P("slab", "sec"), P("slab", "sec"), P("sec"), P(), P("sec", None), P()),
        out_specs=(P("slab", "sec"), P("slab", "sec")),
        check_vma=False,
    )
```

time: 81.1 us -> 56.7 us (0.70)
  starting transfers between devices: 26.4 us -> 0 us
  Pallas kernels: 28.3 us -> 53.7 us
  waiting for transfers between devices: 14.4 us -> 0 us
  other arithmetic: 6.14 us -> 0 us
  local copies, waits for them, and re-layouts: 3.6 us -> 2.27 us
  matrix products: 0.98 us -> 0 us
    ppermute x4 -> x0, starting transfers between devices: 26.4 us -> none  [shift_pair(): return (lax.ppermute(last, axis, up), lax.ppermute(leading, axis, down))]
    pallas_call x2 -> x1, Pallas kernels: 28.3 us -> 53.7 us  [body(): pl.pallas_call(rail_kernel, out_shape=(jax.ShapeDtypeStruct((DEPTH, CELLS...]
    ppermute x4 -> x0, waiting for transfers between devices: 14.4 us -> none  [shift_pair(): return (lax.ppermute(last, axis, up), lax.ppermute(leading, axis, down))]
    unnamed x8 -> x4, local copies, waits for them, and re-layouts: 0.03 us -> 2.27 us
    slice x2 -> x0, other arithmetic: 1.54 us -> none  [the longest x1 0.9 us: body(): pile[:, cells - edge:]]
    reshape x2 -> x0, local copies, waits for them, and re-layouts: 1.52 us -> none  [the longest x1 1.45 us: body(): modal_part.reshape(GROUP, 1, 2 * PADB)]
    broadcast_in_dim x5 -> x0, local copies, waits for them, and re-layouts: 1.41 us -> none  [the longest x4 1.41 us: body(): jnp.broadcast_to(edges.reshape(2, 1, 2, 1), (2, 2, 2, K1))]
    pallas_call x1 -> x0, other arithmetic: 1.4 us -> none  [body(): pl.pallas_call(filter_kernel, out_shape=jax.ShapeDtypeStruct((GROUP, 1, 2...]
  transfers between devices with their start and end apart: 4 -> 0, of which waited for: 2 -> 0; matrix products, arithmetic and copies ran while one was open for 3% -> 0% of each run, Pallas kernels for 0% -> 0%
where the time goes in v3:
time: 56.7 us; the launch traced here: 56.6 us
  Pallas kernels  53.7 us (95%)
  local copies, waits for them, and re-layouts  2.27 us (4%)
  between operations  0.65 us (1%)
    pallas_call x1, Pallas kernels, body(): pl.pallas_call(rail_kernel, out_shape=(jax.ShapeDtypeStruct((DEPTH, CELLS...  53.7 us
    unnamed x4, local copies, waits for them, and re-layouts  2.27 us

profile of v3, /device:TPU:1, one launch (start us, length us, event | category | flops | bytes accessed | tf_op | source)
XLA Modules:
  0.0 56.6 jit_solution(16556234213873984647)
XLA Ops:
  0.6 53.7 %shard_map.131 = (f32[40,1024]{1,0:T(8,128)}, bf16[40,1024]{1,0:T(8,128)(2,1)}) custom-call(f32[40,1024]{1,0:T(8,128)} %disp_ref.1, f32[40,1024]{1,0:T(8,128)} %earlier_ref.1, s32[1,1024]{1,0:T(1,128)} %bitcast.3, f32[2,8]{1,0:T(2,128)} %material_ref.1, s32[2,64]{1,0:T(2,128)} %edges_ref.1, f32[64,1024]{1,0:T(8,128)} %bitcast.2, ...), custom_call_target="tpu_custom_call" | custom-call | tf_op jit(solution)/shard_map/pallas_call | solution.py:257
  54.3 0.0 copy-start
  54.3 1.6 %copy.16 = f32[40,1024]{1,0:T(8,128)} copy(f32[40,1024]{1,0:T(8,128)} %get-tuple-element.4) | data formatting | bytes 327680
  55.9 0.0 copy-done
  55.9 0.6 %copy.17 = bf16[40,1024]{1,0:T(8,128)(2,1)} copy(bf16[40,1024]{1,0:T(8,128)(2,1)S(1)} %copy-done) | data formatting | bytes 163840
Async XLA Ops:
  54.3 1.6 %copy-start = (bf16[40,1024]{1,0:T(8,128)(2,1)S(1)}, bf16[40,1024]{1,0:T(8,128)(2,1)}, u32[]{:S(2)}) copy-start(bf16[40,1024]{1,0:T(8,128)(2,1)} %get-tuple-element.5) | copy-start | bytes 245764

commit v4 on v3

--- a/solution.py
+++ b/solution.py
@@ -62,10 +62,11 @@
 
 
 def rail_kernel(
-    disp_ref, earlier_ref, region_ref, material_ref, edges_ref, shapes_ref,
-    rows_ref, dft_ref, twc_ref, tws_ref, fwd_ref, inv_ref,
+    disp_ref, earlier_ref, region_ref, material_ref, edges_ref, shapes_hbm,
+    rows_hbm, dft_hbm, twc_hbm, tws_hbm, fwd_hbm, inv_hbm,
     out_ref, band_ref,
-    stiff_ref, wide, modal_ref, pieces, mine, held, sent, smooth_ref,
+    shapes_ref, rows_ref, dft_ref, twc_ref, tws_ref, fwd_ref, inv_ref, table_sem,
+    blank_ref, stiff_ref, wide, modal_ref, pieces, mine, held, sent, smooth_ref,
     send0, recv0, send1, recv1, send2, recv2, send3, recv3,
 ):
     slab = lax.axis_index("slab")
@@ -89,6 +90,16 @@
 
     barrier = pltpu.get_barrier_semaphore()
 
+    tables = [
+        pltpu.make_async_copy(src, dst, table_sem.at[i])
+        for i, (src, dst) in enumerate(
+            (
+                (shapes_hbm, shapes_ref), (rows_hbm.at[place], rows_ref), (dft_hbm, dft_ref),
+                (twc_hbm, twc_ref), (tws_hbm, tws_ref), (fwd_hbm, fwd_ref), (inv_hbm, inv_ref),
+            )
+        )
+    ]
+
     @pl.loop(1, GROUP)
     def _(step):
         pl.semaphore_signal(barrier, inc=1, device_id=in_group(step)[2], device_id_type=MESH)
@@ -100,12 +111,17 @@
     for up, across in BESIDE:
         pl.semaphore_signal(barrier, inc=1, device_id=beside(up, across), device_id_type=MESH)
 
+    for table in tables:
+        table.start()
     stiff = jnp.zeros((8, CELLS_HERE), jnp.float32)
     region = jnp.broadcast_to(region_ref[...], (8, CELLS_HERE))
     for r in range(REGIONS):
         value = courant_sq * material_ref[0, r] * material_ref[1, r]
         stiff = jnp.where(region == r, value, stiff)
     stiff_ref[...] = stiff
+    blank_ref[...] = jnp.zeros((DEPTH, EDGE), jnp.float32)
+    for at in (0, TALL - STEPS, TALL, 2 * TALL - STEPS):
+        wide[at : at + STEPS, :] = jnp.zeros((STEPS, BROAD), jnp.float32)
 
     pl.semaphore_wait(barrier, GROUP + PLACES - 2 + len(BESIDE))
 
@@ -123,26 +139,35 @@
             src_ref=src, dst_ref=dst, send_sem=send0.at[len(halo_copies)], recv_sem=recv0,
             device_id=beside(up, across), device_id_type=MESH,
         )
-        copy.start()
-        halo_copies.append(copy)
+        reach = {-1: sec > 0, 0: None, 1: sec < SECS - 1}[across]
+        halo_copies.append((copy, reach))
+        if across == 0:
+            copy.start()
+            return
+        pl.when(reach)(copy.start)
+        lacking = sec == 0 if across == 1 else sec == SECS - 1
+        zeros = blank_ref.at[pl.ds(0, src_rows[1]), :]
+        pl.when(lacking)(pltpu.make_async_copy(zeros, dst, recv0).start)
 
     for up, across in BESIDE + ((0, 0),):
         src_rows, dst_rows = {
-            -1: ((0, PAD), PAD + DEPTH), 1: ((DEPTH - PAD, PAD), 0), 0: ((0, DEPTH), PAD)
+            -1: ((0, STEPS), PAD + DEPTH),
+            1: ((DEPTH - STEPS, STEPS), PAD - STEPS),
+            0: ((0, DEPTH), PAD),
         }[up]
         send_halo(disp_ref, 0, src_rows, dst_rows, up, across)
         send_halo(earlier_ref, TALL, src_rows, dst_rows, up, across)
         if up == 0:
             send_halo(stiff_ref, 2 * TALL, (0, PAD), 0, up, across)
-    pltpu.make_async_copy(wide, wide, recv0).wait()
+    for table in tables:
+        table.wait()
+    arrived = wide.at[pl.ds(0, 2 * (DEPTH + 2 * STEPS) + PAD), :]
+    pltpu.make_async_copy(arrived, arrived, recv0).wait()
 
     lane = lax.broadcasted_iota(jnp.int32, (1, BROAD), 1)
-    start = jnp.where(sec == 0, EDGE, 0)
-    stop = jnp.where(sec == SECS - 1, EDGE + CELLS_HERE, BROAD)
-    inside = (lane >= start) & (lane < stop)
-    current = jnp.where(inside, wide[:TALL, :], 0.0)
-    before = jnp.where(inside, wide[TALL : 2 * TALL, :], 0.0)
-    stiff = jnp.where(inside, wide[2 * TALL : 2 * TALL + 1, :], 0.0)
+    current = wide[:TALL, :]
+    before = wide[TALL : 2 * TALL, :]
+    stiff = wide[2 * TALL : 2 * TALL + 1, :]
     not_first = lane % COLS > 0
     not_last = lane % COLS < COLS - 1
     for _ in range(STEPS):
@@ -160,22 +185,13 @@
     final = current[PAD : PAD + DEPTH, EDGE : EDGE + CELLS_HERE]
     out_ref[...] = final
     lanes = 2 * PADB
-    front = shapes_ref[:GROUP, :]
-    back_half = shapes_ref[GROUP:, :]
-
-    def dot_rows(shapes, planes):
-        return lax.dot_general(
-            shapes, planes, (((1,), (1,)), ((), ())),
-            precision=HIGHEST, preferred_element_type=jnp.float32,
-        )
-
-    def blank(count):
-        return jnp.zeros((count, CELLS_HERE), jnp.float32)
-
-    modal = dot_rows(front, jnp.concatenate([final, blank(lanes - DEPTH)], axis=0))
-    modal = modal + dot_rows(
-        back_half, jnp.concatenate([blank(PADB), final, blank(PADB - DEPTH)], axis=0)
+    shapes = shapes_ref[...]
+    padded = jnp.concatenate([final, jnp.zeros((lanes - DEPTH, CELLS_HERE), jnp.float32)], axis=0)
+    modal = lax.dot_general(
+        shapes, padded, (((1,), (1,)), ((), ())),
+        precision=HIGHEST, preferred_element_type=jnp.float32,
     )
+    modal = modal[:GROUP] + pltpu.roll(modal[GROUP:], PADB, 1)
     for i in range(GROUP):
         modal_ref[i] = modal[i : i + 1, :]
 
@@ -222,7 +238,7 @@
     back = dot(filtered, inv_ref[...])
     real, imag = back[:, :lanes], back[:, lanes:]
     twisted = jnp.concatenate([real * twc - imag * tws, imag * twc + real * tws], axis=0)
-    smooth = dot(rows_ref[place], twisted)
+    smooth = dot(rows_ref[...], twisted)
     for i in range(ZS):
         sent[i] = smooth[i : i + 1, :]
 
@@ -236,11 +252,15 @@
 
     pltpu.make_async_copy(sent.at[z], smooth_ref.at[group], recv3).start()
     pltpu.make_async_copy(smooth_ref, smooth_ref, recv3).wait()
-    gathered = smooth_ref[:, 0, :].T
-    band = dot(gathered[:DEPTH], front) + dot(gathered[PADB : PADB + DEPTH], back_half)
+    gathered = smooth_ref[:, 0, :]
+    gathered = jnp.concatenate([gathered, pltpu.roll(gathered, PADB, 1)], axis=0).T
+    band = dot(gathered[:DEPTH], shapes)
     band_ref[...] = band.astype(jnp.bfloat16)
-    for copy in halo_copies:
-        copy.wait_send()
+    for copy, reach in halo_copies:
+        if reach is None:
+            copy.wait_send()
+        else:
+            pl.when(reach)(copy.wait_send)
     most = pieces.at[pl.ds(0, GROUP - 1)]
     pltpu.make_async_copy(most, most, send1).wait()
     most = held.at[pl.ds(0, PLACES - 1)]
@@ -260,9 +280,14 @@
             jax.ShapeDtypeStruct((DEPTH, CELLS_HERE), jnp.float32),
             jax.ShapeDtypeStruct((DEPTH, CELLS_HERE), jnp.bfloat16),
         ),
-        in_specs=[vmem] * 3 + [smem] * 2 + [vmem] * 7,
+        in_specs=[vmem] * 3 + [smem] * 2 + [pl.BlockSpec(memory_space=pl.ANY)] * 7,
         out_specs=(vmem, vmem),
         scratch_shapes=[
+            pltpu.VMEM((MODES, CELLS_HERE), jnp.float32),
+            pltpu.VMEM(TABLES[0].shape[1:], jnp.float32),
+            *[pltpu.VMEM(t.shape, jnp.float32) for t in TABLES[1:]],
+            dma((7,)),
+            pltpu.VMEM((DEPTH, EDGE), jnp.float32),
             pltpu.VMEM((PAD, CELLS_HERE), jnp.float32),
             pltpu.VMEM((2 * TALL + PAD, BROAD), jnp.float32),
             pltpu.VMEM((GROUP, 1, lanes), jnp.float32),

time: 56.7 us -> 52.4 us (0.924)
  Pallas kernels: 53.7 us -> 49.3 us
    pallas_call x1, Pallas kernels: 53.7 us -> 49.3 us  [body(): pl.pallas_call(rail_kernel, out_shape=(jax.ShapeDtypeStruct((DEPTH, CELLS...]
where the time goes in v4:
time: 52.4 us; the launch traced here: 52.2 us
  Pallas kernels  49.3 us (94%)
  local copies, waits for them, and re-layouts  2.27 us (4%)
  between operations  0.65 us (1%)
    pallas_call x1, Pallas kernels, body(): pl.pallas_call(rail_kernel, out_shape=(jax.ShapeDtypeStruct((DEPTH, CELLS...  49.3 us
    unnamed x4, local copies, waits for them, and re-layouts  2.27 us

profile of v4, /device:TPU:1, one launch (start us, length us, event | category | flops | bytes accessed | tf_op | source)
XLA Modules:
  0.0 52.2 jit_solution(5882039047650943883)
XLA Ops:
  0.6 49.3 %shard_map.131 = (f32[40,1024]{1,0:T(8,128)}, bf16[40,1024]{1,0:T(8,128)(2,1)}) custom-call(f32[40,1024]{1,0:T(8,128)} %disp_ref.1, f32[40,1024]{1,0:T(8,128)} %earlier_ref.1, s32[1,1024]{1,0:T(1,128)} %bitcast.3, f32[2,8]{1,0:T(2,128)} %material_ref.1, s32[2,64]{1,0:T(2,128)} %edges_ref.1, f32[64,1024]{1,0:T(8,128)} %bitcast.2, ...), custom_call_target="tpu_custom_call" | custom-call | tf_op jit(solution)/shard_map/pallas_call | solution.py:277
  49.9 0.0 copy-start
  49.9 1.6 %copy.16 = f32[40,1024]{1,0:T(8,128)} copy(f32[40,1024]{1,0:T(8,128)} %get-tuple-element.4) | data formatting | bytes 327680
  51.6 0.0 copy-done
  51.6 0.6 %copy.17 = bf16[40,1024]{1,0:T(8,128)(2,1)} copy(bf16[40,1024]{1,0:T(8,128)(2,1)S(1)} %copy-done) | data formatting | bytes 163840
Async XLA Ops:
  49.9 1.6 %copy-start = (bf16[40,1024]{1,0:T(8,128)(2,1)S(1)}, bf16[40,1024]{1,0:T(8,128)(2,1)}, u32[]{:S(2)}) copy-start(bf16[40,1024]{1,0:T(8,128)(2,1)} %get-tuple-element.5) | copy-start | bytes 245764

commit v5 on v4

--- a/solution.py
+++ b/solution.py
@@ -33,7 +33,6 @@
 
 courant_sq = 0.14
 two_pi = 2.0 * math.pi
-HIGHEST = lax.Precision.HIGHEST
 
 
 def make_tables():
@@ -61,12 +60,36 @@
 TABLES = make_tables()
 
 
+def far_first(turn, count):
+    return count // 2 + (turn + 1) // 2 * (1 - 2 * (turn % 2))
+
+
+def split(x):
+    high = x.astype(jnp.bfloat16)
+    return high, (x - high.astype(jnp.float32)).astype(jnp.bfloat16)
+
+
+def dot3(x, y, dims=(((1,), (0,)), ((), ()))):
+    (xh, xl), (yh, yl) = split(x), split(y)
+    one = functools.partial(
+        lax.dot_general, dimension_numbers=dims, preferred_element_type=jnp.float32
+    )
+    return one(xh, yh) + (one(xh, yl) + one(xl, yh))
+
+
+def finish_kernel(final_ref, smooth_ref, shapes_ref, out_ref, band_ref):
+    out_ref[...] = final_ref[...]
+    gathered = smooth_ref[:, 0, :]
+    gathered = jnp.concatenate([gathered, pltpu.roll(gathered, PADB, 1)], axis=0).T
+    band_ref[...] = dot3(gathered[:DEPTH], shapes_ref[...]).astype(jnp.bfloat16)
+
+
 def rail_kernel(
     disp_ref, earlier_ref, region_ref, material_ref, edges_ref, shapes_hbm,
     rows_hbm, dft_hbm, twc_hbm, tws_hbm, fwd_hbm, inv_hbm,
-    out_ref, band_ref,
+    out_ref, smooth_ref,
     shapes_ref, rows_ref, dft_ref, twc_ref, tws_ref, fwd_ref, inv_ref, table_sem,
-    blank_ref, stiff_ref, wide, modal_ref, pieces, mine, held, sent, smooth_ref,
+    blank_ref, stiff_ref, wide, modal_ref, pieces, mine, held, sent,
     send0, recv0, send1, recv1, send2, recv2, send3, recv3,
 ):
     slab = lax.axis_index("slab")
@@ -100,12 +123,14 @@
         )
     ]
 
-    @pl.loop(1, GROUP)
-    def _(step):
+    @pl.loop(0, GROUP - 1)
+    def _(turn):
+        step = far_first(turn, GROUP)
         pl.semaphore_signal(barrier, inc=1, device_id=in_group(step)[2], device_id_type=MESH)
 
-    @pl.loop(1, PLACES)
-    def _(step):
+    @pl.loop(0, PLACES - 1)
+    def _(turn):
+        step = far_first(turn, PLACES)
         pl.semaphore_signal(barrier, inc=1, device_id=in_places(step), device_id_type=MESH)
 
     for up, across in BESIDE:
@@ -187,16 +212,14 @@
     lanes = 2 * PADB
     shapes = shapes_ref[...]
     padded = jnp.concatenate([final, jnp.zeros((lanes - DEPTH, CELLS_HERE), jnp.float32)], axis=0)
-    modal = lax.dot_general(
-        shapes, padded, (((1,), (1,)), ((), ())),
-        precision=HIGHEST, preferred_element_type=jnp.float32,
-    )
+    modal = dot3(shapes, padded, (((1,), (1,)), ((), ())))
     modal = modal[:GROUP] + pltpu.roll(modal[GROUP:], PADB, 1)
     for i in range(GROUP):
         modal_ref[i] = modal[i : i + 1, :]
 
-    @pl.loop(1, GROUP)
-    def _(step):
+    @pl.loop(0, GROUP - 1)
+    def _(turn):
+        step = far_first(turn, GROUP)
         other, _, device = in_group(step)
         pltpu.make_async_remote_copy(
             src_ref=modal_ref.at[other], dst_ref=pieces.at[group],
@@ -210,8 +233,9 @@
         total = total + pieces[SECS * i + 2] + pieces[SECS * i + 3]
         mine[i : i + 1, :] = total
 
-    @pl.loop(1, PLACES)
-    def _(step):
+    @pl.loop(0, PLACES - 1)
+    def _(turn):
+        step = far_first(turn, PLACES)
         pltpu.make_async_remote_copy(
             src_ref=mine, dst_ref=held.at[place],
             send_sem=send2, recv_sem=recv2, device_id=in_places(step), device_id_type=MESH,
@@ -220,7 +244,6 @@
     pltpu.make_async_copy(mine, held.at[place], recv2).start()
     pltpu.make_async_copy(held, held, recv2).wait()
 
-    dot = functools.partial(jnp.dot, precision=HIGHEST, preferred_element_type=jnp.float32)
     twc = twc_ref[...]
     tws = tws_ref[...]
     row = lax.broadcasted_iota(jnp.int32, (SLABS, 4 * K1), 0)
@@ -229,21 +252,22 @@
     is_front = lane % (2 * K1) < K1
     lower = jnp.where(is_front, edges_ref[0, group], edges_ref[0, group + GROUP])
     upper = jnp.where(is_front, edges_ref[1, group], edges_ref[1, group + GROUP])
-    both = dot(dft_ref[...], held[...].reshape(SLABS, lanes))
+    both = dot3(dft_ref[...], held[...].reshape(SLABS, lanes))
     real, imag = both[:SLABS], both[SLABS:]
     twisted = jnp.concatenate([real * twc + imag * tws, imag * twc - real * tws], axis=1)
-    spectrum = dot(twisted, fwd_ref[...])
+    spectrum = dot3(twisted, fwd_ref[...])
     in_band = (wave >= lower) & (wave < upper)
     filtered = jnp.where(in_band, spectrum, 0.0)
-    back = dot(filtered, inv_ref[...])
+    back = dot3(filtered, inv_ref[...])
     real, imag = back[:, :lanes], back[:, lanes:]
     twisted = jnp.concatenate([real * twc - imag * tws, imag * twc + real * tws], axis=0)
-    smooth = dot(rows_ref[...], twisted)
+    smooth = dot3(rows_ref[...], twisted)
     for i in range(ZS):
         sent[i] = smooth[i : i + 1, :]
 
-    @pl.loop(1, GROUP)
-    def _(step):
+    @pl.loop(0, GROUP - 1)
+    def _(turn):
+        step = far_first(turn, GROUP)
         _, other_z, device = in_group(step)
         pltpu.make_async_remote_copy(
             src_ref=sent.at[other_z], dst_ref=smooth_ref.at[group],
@@ -252,10 +276,6 @@
 
     pltpu.make_async_copy(sent.at[z], smooth_ref.at[group], recv3).start()
     pltpu.make_async_copy(smooth_ref, smooth_ref, recv3).wait()
-    gathered = smooth_ref[:, 0, :]
-    gathered = jnp.concatenate([gathered, pltpu.roll(gathered, PADB, 1)], axis=0).T
-    band = dot(gathered[:DEPTH], shapes)
-    band_ref[...] = band.astype(jnp.bfloat16)
     for copy, reach in halo_copies:
         if reach is None:
             copy.wait_send()
@@ -274,11 +294,12 @@
     smem = pl.BlockSpec(memory_space=pltpu.SMEM)
     dma = pltpu.SemaphoreType.DMA
     lanes = 2 * PADB
-    return pl.pallas_call(
+    shapes = mode_shapes.T
+    final, smooth = pl.pallas_call(
         rail_kernel,
         out_shape=(
             jax.ShapeDtypeStruct((DEPTH, CELLS_HERE), jnp.float32),
-            jax.ShapeDtypeStruct((DEPTH, CELLS_HERE), jnp.bfloat16),
+            jax.ShapeDtypeStruct((GROUP, 1, lanes), jnp.float32),
         ),
         in_specs=[vmem] * 3 + [smem] * 2 + [pl.BlockSpec(memory_space=pl.ANY)] * 7,
         out_specs=(vmem, vmem),
@@ -295,14 +316,20 @@
             pltpu.VMEM((ZS, lanes), jnp.float32),
             pltpu.VMEM((PLACES, ZS, lanes), jnp.float32),
             pltpu.VMEM((ZS, 1, lanes), jnp.float32),
-            pltpu.VMEM((GROUP, 1, lanes), jnp.float32),
             dma((18,)), dma, dma, dma, dma, dma, dma, dma,
         ],
         compiler_params=pltpu.CompilerParams(collective_id=0, has_side_effects=True),
     )(
         displacement, earlier_field, region_ids.reshape(1, CELLS_HERE), material, band_edges,
-        mode_shapes.T, *[jnp.asarray(t) for t in TABLES],
+        shapes, *[jnp.asarray(t) for t in TABLES],
     )
+    return pl.pallas_call(
+        finish_kernel,
+        out_shape=(
+            jax.ShapeDtypeStruct((DEPTH, CELLS_HERE), jnp.float32),
+            jax.ShapeDtypeStruct((DEPTH, CELLS_HERE), jnp.bfloat16),
+        ),
+    )(final, smooth, shapes)
 
 
 def solution(mesh):

time: 52.4 us -> 51.3 us (0.979)
  local copies, waits for them, and re-layouts: 2.27 us -> 0 us
  Pallas kernels: 49.3 us -> 50.5 us
    unnamed x4 -> x0, local copies, waits for them, and re-layouts: 2.27 us -> none
    pallas_call x0 -> x1, Pallas kernels: none -> 2.04 us  [body(): pl.pallas_call(finish_kernel, out_shape=(jax.ShapeDtypeStruct((DEPTH, CEL...]
    pallas_call x1, Pallas kernels: 49.3 us -> 48.5 us  [body(): pl.pallas_call(rail_kernel, out_shape=(jax.ShapeDtypeStruct((DEPTH, CELLS...]
where the time goes in v5:
time: 51.3 us; the launch traced here: 51.2 us
  Pallas kernels  50.5 us (98%)
  between operations  0.64 us (1%)
    pallas_call x1, Pallas kernels, body(): pl.pallas_call(rail_kernel, out_shape=(jax.ShapeDtypeStruct((DEPTH, CELLS...  48.5 us
    pallas_call x1, Pallas kernels, body(): pl.pallas_call(finish_kernel, out_shape=(jax.ShapeDtypeStruct((DEPTH, CEL...  2.04 us

profile of v5, /device:TPU:1, one launch (start us, length us, event | category | flops | bytes accessed | tf_op | source)
XLA Modules:
  0.0 51.2 jit_solution(3544415365511793300)
XLA Ops:
  0.6 48.5 %shard_map.131 = (f32[40,1024]{1,0:T(8,128)}, f32[32,1,128]{2,1,0:T(1,128)}) custom-call(f32[40,1024]{1,0:T(8,128)} %disp_ref.1, f32[40,1024]{1,0:T(8,128)} %earlier_ref.1, s32[1,1024]{1,0:T(1,128)} %bitcast.4, f32[2,8]{1,0:T(2,128)} %material_ref.1, s32[2,64]{1,0:T(2,128)} %edges_ref.1, f32[64,1024]{1,0:T(8,128)} %bitcast.2, ...), custom_call_target="tpu_custom_call" | custom-call | tf_op jit(solution)/shard_map/pallas_call | solution.py:298
  49.1 2.0 %shard_map.132 = (f32[40,1024]{1,0:T(8,128)}, bf16[40,1024]{1,0:T(8,128)(2,1)}) custom-call(f32[40,1024]{1,0:T(8,128)} %get-tuple-element.4.final_ref, f32[32,1,128]{2,1,0:T(1,128)} %get-tuple-element.5.smooth_ref, f32[64,1024]{1,0:T(8,128)} %bitcast.3), custom_call_target="tpu_custom_call" | custom-call | tf_op jit(solution)/shard_map/pallas_call | solution.py:326

commit v6 on v5

--- a/solution.py
+++ b/solution.py
@@ -26,9 +26,10 @@
 BESIDE = ((0, 1), (0, -1), (1, 0), (-1, 0), (1, 1), (1, -1), (-1, 1), (-1, -1))
 PADB = 64
 K1 = WAVES // SLABS
-ZS = 8
-PLACES = SLABS // ZS
-GROUP = ZS * SECS
+YS = 4
+PLACES = SLABS // YS
+GROUP = YS * SECS
+TILES = 2
 MESH = pl.DeviceIdType.MESH
 
 courant_sq = 0.14
@@ -37,9 +38,13 @@
 
 def make_tables():
     k2 = np.arange(SLABS)
-    held_a = (np.arange(ZS)[None, :] * PLACES + np.arange(PLACES)[:, None]).reshape(-1)
-    first = two_pi * (np.outer(k2, held_a) % SLABS) / SLABS
-    dft_a = np.concatenate([np.cos(first), -np.sin(first)], axis=0)
+    held_a = np.arange(SLABS).reshape(PLACES, 1, YS) + np.zeros((1, TILES, 1), np.int64)
+    first = two_pi * (np.outer(k2, held_a.reshape(-1)) % SLABS) / SLABS
+    held_t = np.broadcast_to(np.arange(TILES)[None, :, None], held_a.shape).reshape(1, -1)
+    own = [held_t == t for t in range(TILES)]
+    dft_a = np.concatenate(
+        [np.cos(first) * m for m in own] + [-np.sin(first) * m for m in own], axis=0
+    )
     b = np.arange(PADB)
     live = (b < DEPTH).astype(np.float64)
     phi = two_pi * np.outer(k2, b) / PLANES
@@ -51,9 +56,12 @@
     s = np.kron(pair, np.sin(psi) * live[:, None])
     forward = np.block([[c, -s], [s, c]])
     inverse = np.block([[c.T, s.T], [-s.T, c.T]])
-    at = held_a.reshape(PLACES, ZS, 1) * k2
-    last = two_pi * (at % SLABS) / SLABS
-    rows = np.concatenate([np.cos(last), -np.sin(last)], axis=2) * (2.0 / PLANES)
+    last = two_pi * (np.arange(SLABS).reshape(PLACES, YS, 1) * k2 % SLABS) / SLABS
+    rows = np.zeros((PLACES, TILES, YS, 2, TILES, SLABS))
+    for t in range(TILES):
+        rows[:, t, :, 0, t] = np.cos(last)
+        rows[:, t, :, 1, t] = -np.sin(last)
+    rows = rows.reshape(PLACES, TILES * YS, 2 * TILES * SLABS) * (2.0 / PLANES)
     return [t.astype(np.float32) for t in (rows, dft_a, tw_cos, tw_sin, forward, inverse)]
 
 
@@ -79,7 +87,7 @@
 
 def finish_kernel(final_ref, smooth_ref, shapes_ref, out_ref, band_ref):
     out_ref[...] = final_ref[...]
-    gathered = smooth_ref[:, 0, :]
+    gathered = jnp.concatenate([smooth_ref[:, t, :] for t in range(TILES)], axis=0)
     gathered = jnp.concatenate([gathered, pltpu.roll(gathered, PADB, 1)], axis=0).T
     band_ref[...] = dot3(gathered[:DEPTH], shapes_ref[...]).astype(jnp.bfloat16)
 
@@ -94,16 +102,16 @@
 ):
     slab = lax.axis_index("slab")
     sec = lax.axis_index("sec")
-    z, place = slab // PLACES, slab % PLACES
-    group = z * SECS + sec
+    place, y = slab // YS, slab % YS
+    group = y * SECS + sec
 
     def in_group(step):
         other = lax.rem(group + step, GROUP)
-        other_z = other // SECS
-        return other, other_z, {"slab": other_z * PLACES + place, "sec": lax.rem(other, SECS)}
+        other_y = other // SECS
+        return other, other_y, {"slab": place * YS + other_y, "sec": lax.rem(other, SECS)}
 
     def in_places(step):
-        return {"slab": z * PLACES + lax.rem(place + step, PLACES), "sec": sec}
+        return {"slab": lax.rem(place + step, PLACES) * YS + y, "sec": sec}
 
     def beside(up, across):
         return {
@@ -213,9 +221,10 @@
     shapes = shapes_ref[...]
     padded = jnp.concatenate([final, jnp.zeros((lanes - DEPTH, CELLS_HERE), jnp.float32)], axis=0)
     modal = dot3(shapes, padded, (((1,), (1,)), ((), ())))
-    modal = modal[:GROUP] + pltpu.roll(modal[GROUP:], PADB, 1)
+    modal = modal[: MODES // 2] + pltpu.roll(modal[MODES // 2 :], PADB, 1)
     for i in range(GROUP):
-        modal_ref[i] = modal[i : i + 1, :]
+        for t in range(TILES):
+            modal_ref[i, t : t + 1, :] = modal[i + GROUP * t : i + GROUP * t + 1, :]
 
     @pl.loop(0, GROUP - 1)
     def _(turn):
@@ -228,10 +237,11 @@
 
     pltpu.make_async_copy(modal_ref.at[group], pieces.at[group], recv1).start()
     pltpu.make_async_copy(pieces, pieces, recv1).wait()
-    for i in range(ZS):
+    for i in range(YS):
         total = pieces[SECS * i] + pieces[SECS * i + 1]
         total = total + pieces[SECS * i + 2] + pieces[SECS * i + 3]
-        mine[i : i + 1, :] = total
+        for t in range(TILES):
+            mine[YS * t + i : YS * t + i + 1, :] = total[t : t + 1, :]
 
     @pl.loop(0, PLACES - 1)
     def _(turn):
@@ -244,37 +254,47 @@
     pltpu.make_async_copy(mine, held.at[place], recv2).start()
     pltpu.make_async_copy(held, held, recv2).wait()
 
-    twc = twc_ref[...]
-    tws = tws_ref[...]
-    row = lax.broadcasted_iota(jnp.int32, (SLABS, 4 * K1), 0)
-    lane = lax.broadcasted_iota(jnp.int32, (SLABS, 4 * K1), 1)
-    wave = row + SLABS * (lane % K1)
+    twc = jnp.concatenate([twc_ref[...]] * TILES, axis=0)
+    tws = jnp.concatenate([tws_ref[...]] * TILES, axis=0)
+    deep = TILES * SLABS
+    row = lax.broadcasted_iota(jnp.int32, (deep, 4 * K1), 0)
+    lane = lax.broadcasted_iota(jnp.int32, (deep, 4 * K1), 1)
+    wave = row % SLABS + SLABS * (lane % K1)
     is_front = lane % (2 * K1) < K1
-    lower = jnp.where(is_front, edges_ref[0, group], edges_ref[0, group + GROUP])
-    upper = jnp.where(is_front, edges_ref[1, group], edges_ref[1, group + GROUP])
-    both = dot3(dft_ref[...], held[...].reshape(SLABS, lanes))
-    real, imag = both[:SLABS], both[SLABS:]
+
+    def edge_of(side):
+        values = []
+        for t in range(TILES):
+            mode = group + GROUP * t
+            values.append(
+                jnp.where(is_front, edges_ref[side, mode], edges_ref[side, mode + MODES // 2])
+            )
+        return jnp.where(row < SLABS, values[0], values[1])
+
+    both = dot3(dft_ref[...], held[...].reshape(deep, lanes))
+    real, imag = both[:deep], both[deep:]
     twisted = jnp.concatenate([real * twc + imag * tws, imag * twc - real * tws], axis=1)
     spectrum = dot3(twisted, fwd_ref[...])
-    in_band = (wave >= lower) & (wave < upper)
+    in_band = (wave >= edge_of(0)) & (wave < edge_of(1))
     filtered = jnp.where(in_band, spectrum, 0.0)
     back = dot3(filtered, inv_ref[...])
     real, imag = back[:, :lanes], back[:, lanes:]
     twisted = jnp.concatenate([real * twc - imag * tws, imag * twc + real * tws], axis=0)
     smooth = dot3(rows_ref[...], twisted)
-    for i in range(ZS):
-        sent[i] = smooth[i : i + 1, :]
+    for i in range(YS):
+        for t in range(TILES):
+            sent[i, t : t + 1, :] = smooth[YS * t + i : YS * t + i + 1, :]
 
     @pl.loop(0, GROUP - 1)
     def _(turn):
         step = far_first(turn, GROUP)
-        _, other_z, device = in_group(step)
+        _, other_y, device = in_group(step)
         pltpu.make_async_remote_copy(
-            src_ref=sent.at[other_z], dst_ref=smooth_ref.at[group],
+            src_ref=sent.at[other_y], dst_ref=smooth_ref.at[group],
             send_sem=send3, recv_sem=recv3, device_id=device, device_id_type=MESH,
         ).start()
 
-    pltpu.make_async_copy(sent.at[z], smooth_ref.at[group], recv3).start()
+    pltpu.make_async_copy(sent.at[y], smooth_ref.at[group], recv3).start()
     pltpu.make_async_copy(smooth_ref, smooth_ref, recv3).wait()
     for copy, reach in halo_copies:
         if reach is None:
@@ -299,7 +319,7 @@
         rail_kernel,
         out_shape=(
             jax.ShapeDtypeStruct((DEPTH, CELLS_HERE), jnp.float32),
-            jax.ShapeDtypeStruct((GROUP, 1, lanes), jnp.float32),
+            jax.ShapeDtypeStruct((GROUP, TILES, lanes), jnp.float32),
         ),
         in_specs=[vmem] * 3 + [smem] * 2 + [pl.BlockSpec(memory_space=pl.ANY)] * 7,
         out_specs=(vmem, vmem),
@@ -311,11 +331,11 @@
             pltpu.VMEM((DEPTH, EDGE), jnp.float32),
             pltpu.VMEM((PAD, CELLS_HERE), jnp.float32),
             pltpu.VMEM((2 * TALL + PAD, BROAD), jnp.float32),
-            pltpu.VMEM((GROUP, 1, lanes), jnp.float32),
-            pltpu.VMEM((GROUP, 1, lanes), jnp.float32),
-            pltpu.VMEM((ZS, lanes), jnp.float32),
-            pltpu.VMEM((PLACES, ZS, lanes), jnp.float32),
-            pltpu.VMEM((ZS, 1, lanes), jnp.float32),
+            pltpu.VMEM((GROUP, TILES, lanes), jnp.float32),
+            pltpu.VMEM((GROUP, TILES, lanes), jnp.float32),
+            pltpu.VMEM((YS * TILES, lanes), jnp.float32),
+            pltpu.VMEM((PLACES, YS * TILES, lanes), jnp.float32),
+            pltpu.VMEM((YS, TILES, lanes), jnp.float32),
             dma((18,)), dma, dma, dma, dma, dma, dma, dma,
         ],
         compiler_params=pltpu.CompilerParams(collective_id=0, has_side_effects=True),

time: 51.3 us -> 47.7 us (0.930)
  Pallas kernels: 50.5 us -> 47 us
    pallas_call x1, Pallas kernels: 48.5 us -> 44.9 us  [body(): pl.pallas_call(rail_kernel, out_shape=(jax.ShapeDtypeStruct((DEPTH, CELLS...]
where the time goes in v6:
time: 47.7 us; the launch traced here: 47.6 us
  Pallas kernels  47 us (99%)
  between operations  0.64 us (1%)
    pallas_call x1, Pallas kernels, body(): pl.pallas_call(rail_kernel, out_shape=(jax.ShapeDtypeStruct((DEPTH, CELLS...  44.9 us
    pallas_call x1, Pallas kernels, body(): pl.pallas_call(finish_kernel, out_shape=(jax.ShapeDtypeStruct((DEPTH, CEL...  2.03 us

profile of v6, /device:TPU:1, one launch (start us, length us, event | category | flops | bytes accessed | tf_op | source)
XLA Modules:
  0.0 47.6 jit_solution(6426789197772775115)
XLA Ops:
  0.6 44.9 %shard_map.131 = (f32[40,1024]{1,0:T(8,128)}, f32[16,2,128]{2,1,0:T(2,128)}) custom-call(f32[40,1024]{1,0:T(8,128)} %disp_ref.1, f32[40,1024]{1,0:T(8,128)} %earlier_ref.1, s32[1,1024]{1,0:T(1,128)} %bitcast.4, f32[2,8]{1,0:T(2,128)} %material_ref.1, s32[2,64]{1,0:T(2,128)} %edges_ref.1, f32[64,1024]{1,0:T(8,128)} %bitcast.2, ...), custom_call_target="tpu_custom_call" | custom-call | tf_op jit(solution)/shard_map/pallas_call | solution.py:318
  45.6 2.0 %shard_map.132 = (f32[40,1024]{1,0:T(8,128)}, bf16[40,1024]{1,0:T(8,128)(2,1)}) custom-call(f32[40,1024]{1,0:T(8,128)} %get-tuple-element.4.final_ref, f32[16,2,128]{2,1,0:T(2,128)} %get-tuple-element.5.smooth_ref, f32[64,1024]{1,0:T(8,128)} %bitcast.3), custom_call_target="tpu_custom_call" | custom-call | tf_op jit(solution)/shard_map/pallas_call | solution.py:346
